TPU v7x, 32 devices: a whole 2x2x4 slice. The times are simulated.
32 devices in a mesh: space: 16 (over z, x, core), mode: 2 (over y).
Axes of the slice: x: 2, y: 2, z: 4, core: 2. Of those that a mesh axis runs over, the one named last changes fastest.
Arguments:
- field: float32 [3, 16, 128, 64, 256], P(None, 'mode', 'space'), may hold values from -6 to 6
- velocity: float32 [128, 64, 256], P('space'), may hold values from 0.1 to 1
- dispersion: float32 [128, 64, 256], P('space'), may hold values from 0.05 to 0.3
- mobility: float32 [3, 8, 16], replicated, may hold values from -0.2 to 0.2
- material: int32 [128, 64, 256], P('space'), may hold values from 0 to 7
- fixed_mask: int32 [128, 64, 256], P('space'), may hold values 0 or 1
Outputs:
- advanced: float32 [3, 16, 128, 64, 256], P(None, 'mode', 'space')
All inputs are finite; a program needn't handle non-finite values. No bound on the sum of `fixed_mask` on one device may be relied on, other than what follows from the above.
Results may differ from a plain program's by a relative error of at most 0.0001.
Values sent between devices are 32-bit elements; how exact they have to be, the bound alone decides.
A program may use at most 128 MiB of HBM per device.

v0:
```python
import math

import jax
import jax.numpy as jnp
from jax import lax
from jax.sharding import PartitionSpec as P

STEPS = 2


TIME_STEP = 0.1
MOBILE_BASE = 0.7


def padded(array, sides, width):
    for axis, dim in sides:
        size, length = (lax.axis_size(axis), array.shape[dim])
        up = [(i, (i + 1) % size) for i in range(size - 1)]
        down = [(j, i) for i, j in up]
        last = lax.slice_in_dim(array, length - width, length, axis=dim)
        first = lax.slice_in_dim(array, 0, width, axis=dim)
        before = lax.ppermute(last, axis, up)
        after = lax.ppermute(first, axis, down)
        array = jnp.concatenate([before, array, after], axis=dim)
    return array


def legendre_weight(order):
    return math.comb(2 * order, order) / 4.0**order


def triple_table(terms_count):
    entries = []
    for degree_a in range(terms_count):
        slab_values = []
        for degree_b in range(terms_count):
            row_values = []
            for degree_c in range(terms_count):
                degree_sum = degree_a + degree_b + degree_c
                halfsum = degree_sum // 2
                amount = 0.0
                if (
                    degree_sum % 2 == 0
                    and halfsum >= degree_a
                    and (halfsum >= degree_b)
                    and (halfsum >= degree_c)
                ):
                    amount = (
                        legendre_weight(halfsum - degree_a)
                        * legendre_weight(halfsum - degree_b)
                        * legendre_weight(halfsum - degree_c)
                    )
                    amount = amount / legendre_weight(halfsum) / (degree_sum + 1)
                    amount = amount * math.sqrt(
                        (2 * degree_a + 1) * (2 * degree_b + 1) * (2 * degree_c + 1)
                    )
                row_values.append(amount)
            slab_values.append(row_values)
        entries.append(slab_values)
    return jnp.asarray(entries, jnp.float32)


def stencil(x_padded, y_padded, velocity, dispersion):
    middle = x_padded[:, :, 2:-2]
    left_two = x_padded[:, :, :-4]
    left_one = x_padded[:, :, 1:-3]
    right_one = x_padded[:, :, 3:-1]
    right_two = x_padded[:, :, 4:]
    lower_y = y_padded[:, :, :, :-2]
    upper_y = y_padded[:, :, :, 2:]
    z_padded = jnp.pad(middle, ((0, 0), (0, 0), (0, 0), (0, 0), (1, 1)))
    lower_z = z_padded[:, :, :, :, :-2]
    upper_z = z_padded[:, :, :, :, 2:]
    spread = (16.0 * (left_one + right_one) - (left_two + right_two) - 30.0 * middle) / 12.0
    spread = spread + (lower_y + upper_y) + (lower_z + upper_z) - 4.0 * middle
    carried = (2.0 * right_one + 3.0 * middle - 6.0 * left_one + left_two) / 6.0
    return dispersion[None, None] * spread - velocity[None, None] * carried


def class_terms(total, class_mats, piece, picks):

    def add_class(klass, running):
        matrix = lax.dynamic_index_in_dim(class_mats, klass, 1, keepdims=False)
        mixed = jnp.einsum("mij,mjxyz->mixyz", matrix, piece, precision=lax.Precision.HIGHEST)
        chosen = lax.dynamic_index_in_dim(picks, klass, 0, keepdims=False)
        return running + chosen[None, None] * mixed

    return lax.fori_loop(0, class_mats.shape[1], add_class, total)


def on_device(field, velocity, dispersion, mobility, material, fixed_mask):
    modes = mobility.shape[2]
    classes = mobility.shape[1]
    triple = triple_table(modes)
    class_mats = jnp.einsum("ijk,mck->mcij", triple, mobility, precision=lax.Precision.HIGHEST)
    mode_count = lax.axis_size("mode")
    mode_index = lax.axis_index("mode")
    rows_local = field.shape[3] // mode_count
    picks = (material[None] == jnp.arange(classes, dtype=jnp.int32)[:, None, None, None]).astype(
        jnp.float32
    )
    movable = (1 - fixed_mask).astype(jnp.float32)

    def rows_of(array, axis):
        return lax.dynamic_slice_in_dim(array, mode_index * rows_local, rows_local, axis)

    state = lax.all_to_all(field, "mode", split_axis=3, concat_axis=1, tiled=True)
    speed_here = rows_of(velocity, 1)
    spread_here = rows_of(dispersion, 1)
    picks_here = rows_of(picks, 2)
    movable_here = rows_of(movable, 1)
    for sweep_index in range(STEPS):
        x_padded = padded(state, (("space", 2),), 2)
        y_padded = padded(state, (("mode", 3),), 1)
        operated = stencil(x_padded, y_padded, speed_here, spread_here)
        coupled = class_terms(MOBILE_BASE * operated, class_mats, operated, picks_here)
        state = state + TIME_STEP * movable_here[None, None] * coupled
    state = lax.all_to_all(state, "mode", split_axis=1, concat_axis=3, tiled=True)
    return state


def solution(mesh):
    in_specs = (
        P(None, "mode", "space", None, None),
        P("space", None, None),
        P("space", None, None),
        P(),
        P("space", None, None),
        P("space", None, None),
    )
    out_specs = P(None, "mode", "space", None, None)
    return jax.shard_map(
        on_device, mesh=mesh, in_specs=in_specs, out_specs=out_specs, check_vma=False
    )
```

profile of v0, /device:TPU:10, one launch (start us, length us, event | category | flops | bytes accessed | tf_op | source)
XLA Modules:
  0.0 968.9 jit_solution(4053792120406774539)
XLA Ops:
  0.0 0.0 copy-start
  0.0 16.7 %copy.12 = f32[3,8,8,64,256]{4,2,1,0,3:T(8,128)} copy(f32[3,8,8,64,256]{4,3,2,1,0:T(8,128)} %param.11) | data formatting | bytes 25165824 | tf_op args[0]
  16.7 152.3 %all_to_all.36 = f32[3,8,8,64,256]{4,2,1,0,3:T(8,128)} all-to-all(f32[3,8,8,64,256]{4,2,1,0,3:T(8,128)} %copy.12), channel_id=1, replica_groups=mesh['space'=16,'mode'=2] {'mode'}, dimensions={3} | all-to-all | bytes 25165824 | tf_op jit(solution)/shard_map/all_to_all | solution.py:107
  169.0 16.6 %copy.13 = f32[3,2,8,8,32,256]{5,4,3,0,2,1:T(8,128)} copy(f32[3,2,8,8,32,256]{5,3,2,0,4,1:T(8,128)} %bitcast.53) | data formatting | bytes 25165824 | tf_op jit(solution)/shard_map/all_to_all | solution.py:107
  185.6 0.0 copy-start.6
  185.6 6.8 fusion.46
  192.4 1.9 collective-permute-start
  194.3 3.6 collective-permute-start.1
  198.0 0.0 copy-done.9
  198.0 0.0 copy-done.10
  198.0 1.0 convolution_bitcast_fusion
  199.1 0.0 copy-done
  199.1 0.0 copy-done.7
  199.1 0.0 copy-done.8
  199.1 0.1 dynamic-slice_multiply_fusion
  199.2 3.6 fusion.47
  202.8 3.0 collective-permute-start.2
  205.8 1.3 collective-permute-start.3
  207.1 0.3 fusion.38
  207.4 6.1 collective-permute-done.2
  213.5 5.0 collective-permute-done.3
  218.5 46.5 %collective-permute-done = f32[3,16,2,32,256]{4,3,2,0,1:T(8,128)} collective-permute-done((f32[3,16,2,32,256]{4,3,2,0,1:T(8,128)}, f32[3,16,2,32,256]{4,3,2,0,1:T(8,128)}, u32[]{:S(2)}, u32[]{:S(2)}) %collective-permute-start) | collective-permute-done | bytes 3145760 | tf_op jit(solution)/shard_map/ppermute | solution.py:22
  265.0 0.0 collective-permute-done.1
  265.0 46.0 %broadcast_multiply_fusion.1 = (f32[3,16,8,32,256]{4,3,2,0,1:T(8,128)}, f32[3,16,8,32,256]{4,3,2,0,1:T(8,128)}) fusion(f32[8,32,256]{2,1,0:T(8,128)S(1)} %get-tuple-element.247, f32[3,16,8,32,256]{4,3,2,0,1:T(8,128)} %bitcast.52, f32[3,16,8,1,256]{4,3,2,0,1:T(1,128)} %collective-permute-done.3, f32[3,16,8,1,256]{4,3,2,0,1:T(1,128)} %collective-permute-done.2, ...), kind=kLoop, calls=%fused_computation.65 | loop fusion | flops 91226112 | bytes 45350912 | tf_op jit(solution)/shard_map/mul | solution.py:116
  311.0 20.3 %copy.14 = f32[3,16,8,32,256]{4,1,3,2,0:T(8,128)} copy(f32[3,16,8,32,256]{4,3,2,0,1:T(8,128)} %get-tuple-element.237) | data formatting | bytes 25165824 | tf_op jit(solution)/shard_map/while | solution.py:88
  331.3 20.4 %copy.16 = f32[3,16,8,32,256]{4,1,3,2,0:T(8,128)} copy(f32[3,16,8,32,256]{4,3,2,0,1:T(8,128)} %get-tuple-element.238) | data formatting | bytes 25165824 | tf_op jit(solution)/shard_map/while | solution.py:88
  351.6 153.1 %while.26 = (s32[]{:T(128)}, f32[3,16,8,32,256]{4,1,3,2,0:T(8,128)}, f32[8,8,32,256]{3,2,1,0:T(8,128)S(1)}, f32[3,8,16,16]{3,2,0,1:T(8,128)S(1)}, f32[3,16,8,32,256]{4,1,3,2,0:T(8,128)}, /*index=5*/s32[]{:T(128)}) while((s32[]{:T(128)}, f32[3,16,8,32,256]{4,1,3,2,0:T(8,128)}, f32[8,8,32,256]{3,2,1,0:T(8,128)S(1)}, ...), condition=%wide.region_1.2_spmd, body=%wide.region_0.1_spmd.sunk | while | flops 610271232 | bytes 38559820 | solution.py:88
  352.0 19.1 %multiply_add_fusion.4 = f32[3,16,8,32,256]{4,1,3,2,0:T(8,128)} fusion(f32[3,16,8,32,256]{4,1,3,2,0:T(8,128)} %get-tuple-element.318, f32[8,32,256]{2,1,0:T(8,128)S(1)} %dynamic-slice_bitcast_fusion.4, f32[3,16,8,32,256]{4,1,3,2,0:T(8,128)} %get-tuple-element.327, f32[3,8,16,16]{3,2,0,1:T(8,128)S(1)} %get-tuple-element.326, s32[]{:T(128)} %get-tuple-element.317), kind=kOutput, calls=%fused_computation.clone.1 | convolution fusion | flops 610271232 | bytes 38035460 | tf_op jit(solution)/shard_map/while/body/eval_jaxpr/mij,mjxyz->mixyz/dot_general | solution.py:84
  371.1 19.1 %multiply_add_fusion.4 = f32[3,16,8,32,256]{4,1,3,2,0:T(8,128)} fusion(f32[3,16,8,32,256]{4,1,3,2,0:T(8,128)} %get-tuple-element.318, f32[8,32,256]{2,1,0:T(8,128)S(1)} %dynamic-slice_bitcast_fusion.4, f32[3,16,8,32,256]{4,1,3,2,0:T(8,128)} %get-tuple-element.327, f32[3,8,16,16]{3,2,0,1:T(8,128)S(1)} %get-tuple-element.326, s32[]{:T(128)} %get-tuple-element.317), kind=kOutput, calls=%fused_computation.clone.1 | convolution fusion | flops 610271232 | bytes 38035460 | tf_op jit(solution)/shard_map/while/body/eval_jaxpr/mij,mjxyz->mixyz/dot_general | solution.py:84
  390.2 19.1 %multiply_add_fusion.4 = f32[3,16,8,32,256]{4,1,3,2,0:T(8,128)} fusion(f32[3,16,8,32,256]{4,1,3,2,0:T(8,128)} %get-tuple-element.318, f32[8,32,256]{2,1,0:T(8,128)S(1)} %dynamic-slice_bitcast_fusion.4, f32[3,16,8,32,256]{4,1,3,2,0:T(8,128)} %get-tuple-element.327, f32[3,8,16,16]{3,2,0,1:T(8,128)S(1)} %get-tuple-element.326, s32[]{:T(128)} %get-tuple-element.317), kind=kOutput, calls=%fused_computation.clone.1 | convolution fusion | flops 610271232 | bytes 38035460 | tf_op jit(solution)/shard_map/while/body/eval_jaxpr/mij,mjxyz->mixyz/dot_general | solution.py:84
  409.3 19.1 %multiply_add_fusion.4 = f32[3,16,8,32,256]{4,1,3,2,0:T(8,128)} fusion(f32[3,16,8,32,256]{4,1,3,2,0:T(8,128)} %get-tuple-element.318, f32[8,32,256]{2,1,0:T(8,128)S(1)} %dynamic-slice_bitcast_fusion.4, f32[3,16,8,32,256]{4,1,3,2,0:T(8,128)} %get-tuple-element.327, f32[3,8,16,16]{3,2,0,1:T(8,128)S(1)} %get-tuple-element.326, s32[]{:T(128)} %get-tuple-element.317), kind=kOutput, calls=%fused_computation.clone.1 | convolution fusion | flops 610271232 | bytes 38035460 | tf_op jit(solution)/shard_map/while/body/eval_jaxpr/mij,mjxyz->mixyz/dot_general | solution.py:84
  428.4 19.1 %multiply_add_fusion.4 = f32[3,16,8,32,256]{4,1,3,2,0:T(8,128)} fusion(f32[3,16,8,32,256]{4,1,3,2,0:T(8,128)} %get-tuple-element.318, f32[8,32,256]{2,1,0:T(8,128)S(1)} %dynamic-slice_bitcast_fusion.4, f32[3,16,8,32,256]{4,1,3,2,0:T(8,128)} %get-tuple-element.327, f32[3,8,16,16]{3,2,0,1:T(8,128)S(1)} %get-tuple-element.326, s32[]{:T(128)} %get-tuple-element.317), kind=kOutput, calls=%fused_computation.clone.1 | convolution fusion | flops 610271232 | bytes 38035460 | tf_op jit(solution)/shard_map/while/body/eval_jaxpr/mij,mjxyz->mixyz/dot_general | solution.py:84
  447.5 19.1 %multiply_add_fusion.4 = f32[3,16,8,32,256]{4,1,3,2,0:T(8,128)} fusion(f32[3,16,8,32,256]{4,1,3,2,0:T(8,128)} %get-tuple-element.318, f32[8,32,256]{2,1,0:T(8,128)S(1)} %dynamic-slice_bitcast_fusion.4, f32[3,16,8,32,256]{4,1,3,2,0:T(8,128)} %get-tuple-element.327, f32[3,8,16,16]{3,2,0,1:T(8,128)S(1)} %get-tuple-element.326, s32[]{:T(128)} %get-tuple-element.317), kind=kOutput, calls=%fused_computation.clone.1 | convolution fusion | flops 610271232 | bytes 38035460 | tf_op jit(solution)/shard_map/while/body/eval_jaxpr/mij,mjxyz->mixyz/dot_general | solution.py:84
  466.6 19.1 %multiply_add_fusion.4 = f32[3,16,8,32,256]{4,1,3,2,0:T(8,128)} fusion(f32[3,16,8,32,256]{4,1,3,2,0:T(8,128)} %get-tuple-element.318, f32[8,32,256]{2,1,0:T(8,128)S(1)} %dynamic-slice_bitcast_fusion.4, f32[3,16,8,32,256]{4,1,3,2,0:T(8,128)} %get-tuple-element.327, f32[3,8,16,16]{3,2,0,1:T(8,128)S(1)} %get-tuple-element.326, s32[]{:T(128)} %get-tuple-element.317), kind=kOutput, calls=%fused_computation.clone.1 | convolution fusion | flops 610271232 | bytes 38035460 | tf_op jit(solution)/shard_map/while/body/eval_jaxpr/mij,mjxyz->mixyz/dot_general | solution.py:84
  485.7 19.1 %multiply_add_fusion.4 = f32[3,16,8,32,256]{4,1,3,2,0:T(8,128)} fusion(f32[3,16,8,32,256]{4,1,3,2,0:T(8,128)} %get-tuple-element.318, f32[8,32,256]{2,1,0:T(8,128)S(1)} %dynamic-slice_bitcast_fusion.4, f32[3,16,8,32,256]{4,1,3,2,0:T(8,128)} %get-tuple-element.327, f32[3,8,16,16]{3,2,0,1:T(8,128)S(1)} %get-tuple-element.326, s32[]{:T(128)} %get-tuple-element.317), kind=kOutput, calls=%fused_computation.clone.1 | convolution fusion | flops 610271232 | bytes 38035460 | tf_op jit(solution)/shard_map/while/body/eval_jaxpr/mij,mjxyz->mixyz/dot_general | solution.py:84
  504.8 13.4 %fusion.37 = f32[3,16,8,32,256]{4,3,2,0,1:T(8,128)S(1)} fusion(f32[3,16,8,32,256]{4,1,3,2,0:T(8,128)} %get-tuple-element.193, f32[8,32,256]{2,1,0:T(8,128)S(1)} %fusion.40, f32[3,2,8,8,32,256]{5,4,3,0,2,1:T(8,128)} %copy.13), kind=kLoop, calls=%fused_computation.63 | loop fusion | flops 6291456 | bytes 38010880 | tf_op jit(solution)/shard_map/add | solution.py:117
  518.2 0.0 copy-start.2
  518.2 1.1 fusion.44
  519.3 1.9 collective-permute-start.4
  521.3 3.6 collective-permute-start.5
  524.9 0.6 fusion.45
  525.5 2.2 collective-permute-start.6
  527.8 1.3 collective-permute-start.7
  529.1 6.0 collective-permute-done.6
  535.0 4.1 collective-permute-done.7
  539.2 52.5 %collective-permute-done.4 = f32[3,16,2,32,256]{4,3,2,0,1:T(8,128)S(1)} collective-permute-done((f32[3,16,2,32,256]{4,3,2,0,1:T(8,128)S(1)}, f32[3,16,2,32,256]{4,3,2,0,1:T(8,128)S(1)}, u32[]{:S(2)}, u32[]{:S(2)}) %collective-permute-start.4) | collective-permute-done | bytes 3145760 | tf_op jit(solution)/shard_map/ppermute | solution.py:22
  591.6 0.0 copy-done.4
  591.6 1.7 copy-done.3
  593.4 0.0 collective-permute-done.5
  593.4 45.7 %broadcast_multiply_fusion = (f32[3,16,8,32,256]{4,3,2,0,1:T(8,128)}, f32[3,16,8,32,256]{4,3,2,0,1:T(8,128)}) fusion(f32[8,32,256]{2,1,0:T(8,128)S(1)} %get-tuple-element.247, f32[3,16,8,32,256]{4,3,2,0,1:T(8,128)} %copy-done.2, f32[3,16,8,1,256]{4,3,2,0,1:T(1,128)} %copy-done.5, f32[3,16,8,1,256]{4,3,2,0,1:T(1,128)} %copy-done.4, ...), kind=kLoop, calls=%fused_computation.64 | loop fusion | flops 91226112 | bytes 45350912 | tf_op jit(solution)/shard_map/mul | solution.py:116
  639.1 20.3 %copy.18 = f32[3,16,8,32,256]{4,1,3,2,0:T(8,128)} copy(f32[3,16,8,32,256]{4,3,2,0,1:T(8,128)} %get-tuple-element.235) | data formatting | bytes 25165824 | tf_op jit(solution)/shard_map/while | solution.py:88
  659.4 20.4 %copy.20 = f32[3,16,8,32,256]{4,1,3,2,0:T(8,128)} copy(f32[3,16,8,32,256]{4,3,2,0,1:T(8,128)} %get-tuple-element.236) | data formatting | bytes 25165824 | tf_op jit(solution)/shard_map/while | solution.py:88
  679.8 153.0 %while.27 = (s32[]{:T(128)}, f32[3,16,8,32,256]{4,1,3,2,0:T(8,128)}, f32[8,8,32,256]{3,2,1,0:T(8,128)S(1)}, f32[3,8,16,16]{3,2,0,1:T(8,128)S(1)}, f32[3,16,8,32,256]{4,1,3,2,0:T(8,128)}, /*index=5*/s32[]{:T(128)}) while((s32[]{:T(128)}, f32[3,16,8,32,256]{4,1,3,2,0:T(8,128)}, f32[8,8,32,256]{3,2,1,0:T(8,128)S(1)}, ...), condition=%wide.region_3.4_spmd, body=%wide.region_2.3_spmd.sunk | while | flops 610271232 | bytes 38559820 | solution.py:88
  680.1 19.1 %multiply_add_fusion.5 = f32[3,16,8,32,256]{4,1,3,2,0:T(8,128)} fusion(f32[3,16,8,32,256]{4,1,3,2,0:T(8,128)} %get-tuple-element.336, f32[8,32,256]{2,1,0:T(8,128)S(1)} %dynamic-slice_bitcast_fusion.5, f32[3,16,8,32,256]{4,1,3,2,0:T(8,128)} %get-tuple-element.345, f32[3,8,16,16]{3,2,0,1:T(8,128)S(1)} %get-tuple-element.344, s32[]{:T(128)} %get-tuple-element.335), kind=kOutput, calls=%fused_computation.5.clone.1 | convolution fusion | flops 610271232 | bytes 38035460 | tf_op jit(solution)/shard_map/while/body/eval_jaxpr/mij,mjxyz->mixyz/dot_general | solution.py:84
  699.2 19.1 %multiply_add_fusion.5 = f32[3,16,8,32,256]{4,1,3,2,0:T(8,128)} fusion(f32[3,16,8,32,256]{4,1,3,2,0:T(8,128)} %get-tuple-element.336, f32[8,32,256]{2,1,0:T(8,128)S(1)} %dynamic-slice_bitcast_fusion.5, f32[3,16,8,32,256]{4,1,3,2,0:T(8,128)} %get-tuple-element.345, f32[3,8,16,16]{3,2,0,1:T(8,128)S(1)} %get-tuple-element.344, s32[]{:T(128)} %get-tuple-element.335), kind=kOutput, calls=%fused_computation.5.clone.1 | convolution fusion | flops 610271232 | bytes 38035460 | tf_op jit(solution)/shard_map/while/body/eval_jaxpr/mij,mjxyz->mixyz/dot_general | solution.py:84
  718.2 19.1 %multiply_add_fusion.5 = f32[3,16,8,32,256]{4,1,3,2,0:T(8,128)} fusion(f32[3,16,8,32,256]{4,1,3,2,0:T(8,128)} %get-tuple-element.336, f32[8,32,256]{2,1,0:T(8,128)S(1)} %dynamic-slice_bitcast_fusion.5, f32[3,16,8,32,256]{4,1,3,2,0:T(8,128)} %get-tuple-element.345, f32[3,8,16,16]{3,2,0,1:T(8,128)S(1)} %get-tuple-element.344, s32[]{:T(128)} %get-tuple-element.335), kind=kOutput, calls=%fused_computation.5.clone.1 | convolution fusion | flops 610271232 | bytes 38035460 | tf_op jit(solution)/shard_map/while/body/eval_jaxpr/mij,mjxyz->mixyz/dot_general | solution.py:84
  737.3 19.1 %multiply_add_fusion.5 = f32[3,16,8,32,256]{4,1,3,2,0:T(8,128)} fusion(f32[3,16,8,32,256]{4,1,3,2,0:T(8,128)} %get-tuple-element.336, f32[8,32,256]{2,1,0:T(8,128)S(1)} %dynamic-slice_bitcast_fusion.5, f32[3,16,8,32,256]{4,1,3,2,0:T(8,128)} %get-tuple-element.345, f32[3,8,16,16]{3,2,0,1:T(8,128)S(1)} %get-tuple-element.344, s32[]{:T(128)} %get-tuple-element.335), kind=kOutput, calls=%fused_computation.5.clone.1 | convolution fusion | flops 610271232 | bytes 38035460 | tf_op jit(solution)/shard_map/while/body/eval_jaxpr/mij,mjxyz->mixyz/dot_general | solution.py:84
  756.4 19.1 %multiply_add_fusion.5 = f32[3,16,8,32,256]{4,1,3,2,0:T(8,128)} fusion(f32[3,16,8,32,256]{4,1,3,2,0:T(8,128)} %get-tuple-element.336, f32[8,32,256]{2,1,0:T(8,128)S(1)} %dynamic-slice_bitcast_fusion.5, f32[3,16,8,32,256]{4,1,3,2,0:T(8,128)} %get-tuple-element.345, f32[3,8,16,16]{3,2,0,1:T(8,128)S(1)} %get-tuple-element.344, s32[]{:T(128)} %get-tuple-element.335), kind=kOutput, calls=%fused_computation.5.clone.1 | convolution fusion | flops 610271232 | bytes 38035460 | tf_op jit(solution)/shard_map/while/body/eval_jaxpr/mij,mjxyz->mixyz/dot_general | solution.py:84
  775.5 19.1 %multiply_add_fusion.5 = f32[3,16,8,32,256]{4,1,3,2,0:T(8,128)} fusion(f32[3,16,8,32,256]{4,1,3,2,0:T(8,128)} %get-tuple-element.336, f32[8,32,256]{2,1,0:T(8,128)S(1)} %dynamic-slice_bitcast_fusion.5, f32[3,16,8,32,256]{4,1,3,2,0:T(8,128)} %get-tuple-element.345, f32[3,8,16,16]{3,2,0,1:T(8,128)S(1)} %get-tuple-element.344, s32[]{:T(128)} %get-tuple-element.335), kind=kOutput, calls=%fused_computation.5.clone.1 | convolution fusion | flops 610271232 | bytes 38035460 | tf_op jit(solution)/shard_map/while/body/eval_jaxpr/mij,mjxyz->mixyz/dot_general | solution.py:84
  794.6 19.1 %multiply_add_fusion.5 = f32[3,16,8,32,256]{4,1,3,2,0:T(8,128)} fusion(f32[3,16,8,32,256]{4,1,3,2,0:T(8,128)} %get-tuple-element.336, f32[8,32,256]{2,1,0:T(8,128)S(1)} %dynamic-slice_bitcast_fusion.5, f32[3,16,8,32,256]{4,1,3,2,0:T(8,128)} %get-tuple-element.345, f32[3,8,16,16]{3,2,0,1:T(8,128)S(1)} %get-tuple-element.344, s32[]{:T(128)} %get-tuple-element.335), kind=kOutput, calls=%fused_computation.5.clone.1 | convolution fusion | flops 610271232 | bytes 38035460 | tf_op jit(solution)/shard_map/while/body/eval_jaxpr/mij,mjxyz->mixyz/dot_general | solution.py:84
  813.7 19.1 %multiply_add_fusion.5 = f32[3,16,8,32,256]{4,1,3,2,0:T(8,128)} fusion(f32[3,16,8,32,256]{4,1,3,2,0:T(8,128)} %get-tuple-element.336, f32[8,32,256]{2,1,0:T(8,128)S(1)} %dynamic-slice_bitcast_fusion.5, f32[3,16,8,32,256]{4,1,3,2,0:T(8,128)} %get-tuple-element.345, f32[3,8,16,16]{3,2,0,1:T(8,128)S(1)} %get-tuple-element.344, s32[]{:T(128)} %get-tuple-element.335), kind=kOutput, calls=%fused_computation.5.clone.1 | convolution fusion | flops 610271232 | bytes 38035460 | tf_op jit(solution)/shard_map/while/body/eval_jaxpr/mij,mjxyz->mixyz/dot_general | solution.py:84
  832.8 13.4 %fusion.36 = f32[3,16,8,32,256]{4,3,2,0,1:T(8,128)S(1)} fusion(f32[3,16,8,32,256]{4,3,2,0,1:T(8,128)} %copy-done.2, f32[3,16,8,32,256]{4,1,3,2,0:T(8,128)} %get-tuple-element.194, f32[8,32,256]{2,1,0:T(8,128)S(1)} %fusion.40), kind=kLoop, calls=%fused_computation.61 | loop fusion | flops 6291456 | bytes 38010880 | tf_op jit(solution)/shard_map/add | solution.py:117
  846.2 110.0 %all_to_all.37 = f32[3,16,8,32,256]{4,3,2,0,1:T(8,128)} all-to-all(f32[3,16,8,32,256]{4,3,2,0,1:T(8,128)S(1)} %fusion.36), channel_id=1, replica_groups=mesh['space'=16,'mode'=2] {'mode'}, dimensions={1} | all-to-all | bytes 25165824 | tf_op jit(solution)/shard_map/all_to_all | solution.py:118
  956.3 12.2 %copy.22 = f32[3,8,8,2,32,256]{5,4,3,2,1,0:T(8,128)} copy(f32[3,8,8,2,32,256]{5,4,2,0,1,3:T(8,128)} %bitcast.54) | data formatting | bytes 25165824 | tf_op jit(solution)/shard_map/all_to_all | solution.py:118
  (31 shorter events, 0.4 us)
Async XLA Ops:
  0.0 199.1 %copy-start = (s32[8,64,256]{2,1,0:T(8,128)S(1)}, s32[8,64,256]{2,1,0:T(8,128)}, u32[]{:S(2)}) copy-start(s32[8,64,256]{2,1,0:T(8,128)} %param.15) | copy-start | bytes 1572868
  185.6 12.3 %copy-start.9 = (f32[16,16,16,1]{2,1,3,0:T(8,128)S(1)}, f32[16,16,16,1]{2,1,3,0:T(8,128)}, u32[]{:S(2)}) copy-start(f32[16,16,16,1]{2,1,3,0:T(8,128)} %constant.101) | copy-start | bytes 49156
  185.6 12.4 %copy-start.10 = (f32[3,8,16]{2,1,0:T(8,128)S(1)}, f32[3,8,16]{2,1,0:T(8,128)}, u32[]{:S(2)}) copy-start(f32[3,8,16]{2,1,0:T(8,128)} %param.14) | copy-start | bytes 4612
  185.6 13.5 %copy-start.7 = (f32[8,64,256]{2,1,0:T(8,128)S(1)}, f32[8,64,256]{2,1,0:T(8,128)}, u32[]{:S(2)}) copy-start(f32[8,64,256]{2,1,0:T(8,128)} %param.12) | copy-start | bytes 1572868
  185.6 13.5 %copy-start.8 = (f32[8,64,256]{2,1,0:T(8,128)S(1)}, f32[8,64,256]{2,1,0:T(8,128)}, u32[]{:S(2)}) copy-start(f32[8,64,256]{2,1,0:T(8,128)} %param.13) | copy-start | bytes 1572868
  185.6 21.5 %copy-start.6 = (s32[8,64,256]{2,1,0:T(8,128)S(1)}, s32[8,64,256]{2,1,0:T(8,128)}, u32[]{:S(2)}) copy-start(s32[8,64,256]{2,1,0:T(8,128)} %param.16) | copy-start | bytes 1572868
  192.4 72.6 %collective-permute-start = (f32[3,16,2,32,256]{4,3,2,0,1:T(8,128)}, f32[3,16,2,32,256]{4,3,2,0,1:T(8,128)}, u32[]{:S(2)}, u32[]{:S(2)}) collective-permute-start(f32[3,16,2,32,256]{4,3,2,0,1:T(8,128)} %get-tuple-element.243), channel_id=1, source_target_pairs={{0,2},{2,4},{4,6},{6,8},{8,10},{10,12},{12,14},{14,16},{16,18},{18... | collective-permute-start | bytes 9437192 | tf_op jit(solution)/shard_map/ppermute | solution.py:22
  194.3 70.7 %collective-permute-start.1 = (f32[3,16,2,32,256]{4,3,2,0,1:T(8,128)}, f32[3,16,2,32,256]{4,3,2,0,1:T(8,128)}, u32[]{:S(2)}, u32[]{:S(2)}) collective-permute-start(f32[3,16,2,32,256]{4,3,2,0,1:T(8,128)} %get-tuple-element.244), channel_id=1, source_target_pairs={{2,0},{4,2},{6,4},{8,6},{10,8},{12,10},{14,12},{16,14},{18,16},{20... | collective-permute-start | bytes 9437192 | tf_op jit(solution)/shard_map/ppermute | solution.py:23
  202.8 10.7 %collective-permute-start.2 = (f32[3,16,8,1,256]{4,3,2,0,1:T(1,128)S(1)}, f32[3,16,8,1,256]{4,3,2,0,1:T(1,128)}, u32[]{:S(2)}, u32[]{:S(2)}) collective-permute-start(f32[3,16,8,1,256]{4,3,2,0,1:T(1,128)S(1)} %get-tuple-element.245), channel_id=1, source_target_pairs={{0,1},{2,3},{4,5},{6,7},{8,9},{10,11},{12,13},{14,15},{16,17},{18,... | collective-permute-start | bytes 1179656 | tf_op jit(solution)/shard_map/ppermute | solution.py:22
  205.8 12.7 %collective-permute-start.3 = (f32[3,16,8,1,256]{4,3,2,0,1:T(1,128)S(1)}, f32[3,16,8,1,256]{4,3,2,0,1:T(1,128)}, u32[]{:S(2)}, u32[]{:S(2)}) collective-permute-start(f32[3,16,8,1,256]{4,3,2,0,1:T(1,128)S(1)} %get-tuple-element.246), channel_id=1, source_target_pairs={{1,0},{3,2},{5,4},{7,6},{9,8},{11,10},{13,12},{15,14},{17,16},{19,... | collective-permute-start | bytes 1179656 | tf_op jit(solution)/shard_map/ppermute | solution.py:23
  518.2 6.7 copy-start.2
  519.3 72.3 %collective-permute-start.4 = (f32[3,16,2,32,256]{4,3,2,0,1:T(8,128)S(1)}, f32[3,16,2,32,256]{4,3,2,0,1:T(8,128)S(1)}, u32[]{:S(2)}, u32[]{:S(2)}) collective-permute-start(f32[3,16,2,32,256]{4,3,2,0,1:T(8,128)S(1)} %get-tuple-element.239), channel_id=1, source_target_pairs={{0,2},{2,4},{4,6},{6,8},{8,10},{10,12},{12,14},{14,16},{16,18},{18... | collective-permute-start | bytes 9437192 | tf_op jit(solution)/shard_map/ppermute | solution.py:22
  521.3 72.1 %collective-permute-start.5 = (f32[3,16,2,32,256]{4,3,2,0,1:T(8,128)S(1)}, f32[3,16,2,32,256]{4,3,2,0,1:T(8,128)}, u32[]{:S(2)}, u32[]{:S(2)}) collective-permute-start(f32[3,16,2,32,256]{4,3,2,0,1:T(8,128)S(1)} %get-tuple-element.240), channel_id=1, source_target_pairs={{2,0},{4,2},{6,4},{8,6},{10,8},{12,10},{14,12},{16,14},{18,16},{20... | collective-permute-start | bytes 9437192 | tf_op jit(solution)/shard_map/ppermute | solution.py:23
  525.5 9.5 collective-permute-start.6
  527.8 11.4 %collective-permute-start.7 = (f32[3,16,8,1,256]{4,3,2,0,1:T(1,128)S(1)}, f32[3,16,8,1,256]{4,3,2,0,1:T(1,128)S(1)}, u32[]{:S(2)}, u32[]{:S(2)}) collective-permute-start(f32[3,16,8,1,256]{4,3,2,0,1:T(1,128)S(1)} %get-tuple-element.242), channel_id=1, source_target_pairs={{1,0},{3,2},{5,4},{7,6},{9,8},{11,10},{13,12},{15,14},{17,16},{19,... | collective-permute-start | bytes 1179656 | tf_op jit(solution)/shard_map/ppermute | solution.py:23
  535.0 56.6 %copy-start.4 = (f32[3,16,8,1,256]{4,3,2,0,1:T(1,128)}, f32[3,16,8,1,256]{4,3,2,0,1:T(1,128)S(1)}, u32[]{:S(2)}) copy-start(f32[3,16,8,1,256]{4,3,2,0,1:T(1,128)S(1)} %collective-permute-done.6) | copy-start | bytes 1179652
  539.2 52.5 %copy-start.5 = (f32[3,16,8,1,256]{4,3,2,0,1:T(1,128)}, f32[3,16,8,1,256]{4,3,2,0,1:T(1,128)S(1)}, u32[]{:S(2)}) copy-start(f32[3,16,8,1,256]{4,3,2,0,1:T(1,128)S(1)} %collective-permute-done.7) | copy-start | bytes 1179652
  591.6 1.7 copy-start.3
  956.3 12.2 %copy-start.1 = (s32[8,64,256]{2,1,0:T(8,128)S(1)}, s32[8,64,256]{2,1,0:T(8,128)}, u32[]{:S(2)}) copy-start(s32[8,64,256]{2,1,0:T(8,128)} %param.15) | copy-start | bytes 1572868
where the time goes:
time: 975 us; the launch traced here: 969 us
  matrix products  306 us (31%)
  blocking collectives  262 us (27%)
  local copies, waits for them, and re-layouts  141 us (14%)
  waiting for transfers between devices  120 us (12%)
  other arithmetic  119 us (12%)
  starting transfers between devices  18.9 us (2%)
    dot_general x16, matrix products, add_class(): jnp.einsum('mij,mjxyz->mixyz', matrix, piece, precision=lax.Precision.HIG...  305 us
    all_to_all x1, blocking collectives, on_device(): lax.all_to_all(field, 'mode', split_axis=3, concat_axis=1, tiled=True)  152 us
    ppermute x4, waiting for transfers between devices, padded(): before = lax.ppermute(last, axis, up)  111 us
    all_to_all x1, blocking collectives, on_device(): lax.all_to_all(state, 'mode', split_axis=1, concat_axis=3, tiled=True)  110 us
    mul x2, other arithmetic, on_device(): MOBILE_BASE * operated  91.7 us
    while x5, local copies, waits for them, and re-layouts, class_terms(): return lax.fori_loop(0, class_mats.shape[1], add_class, total)  81.4 us
    add x2, other arithmetic, on_device(): state = state + TIME_STEP * movable_here[None, None] * coupled  26.9 us
  transfers between devices with their start and end apart: 8, of which 6 were waited for; matrix products, arithmetic and copies ran while one was open for 1% of the time, Pallas kernels for 0%

commit v1 on v0

v1 whole, which is shorter than its diff:
```python
import functools

import jax
import jax.numpy as jnp
import numpy as np
from jax import lax
from jax.experimental import pallas as pl
from jax.experimental.pallas import tpu as pltpu
from jax.sharding import PartitionSpec as P

STEPS = 2
TIME_STEP = 0.1
MOBILE_BASE = 0.7
TILE = 8


def quadrature(modes):
    pairs = (3 * (modes - 1) + 2) // 4 + 1
    nodes, weights = np.polynomial.legendre.leggauss(2 * pairs)
    nodes, weights = nodes[pairs:], weights[pairs:] / 2
    scale = np.sqrt(2 * np.arange(modes) + 1.0)
    plus = np.polynomial.legendre.legvander(nodes, modes - 1) * scale
    minus = np.polynomial.legendre.legvander(-nodes, modes - 1) * scale
    return plus, minus, weights


def split_rows(matrix):
    big = np.kron(matrix, np.eye(TILE))
    high = big.astype(jnp.bfloat16)
    low = (big - high.astype(np.float64)).astype(jnp.bfloat16)
    return np.concatenate([high, high, low], axis=1)


def tables(modes, mode_count):
    plus, _, weights = quadrature(modes)
    width = modes // mode_count
    out = []
    for q in range(mode_count):
        order = np.concatenate(
            [np.arange(width) + ((q - d) % mode_count) * width for d in range(mode_count)]
        )
        local = plus[:, order]
        back = (local * weights[:, None]).T
        out.append(
            [
                split_rows(local[:, 0::2]),
                split_rows(local[:, 1::2]),
                split_rows(back[0::2]),
                split_rows(back[1::2]),
            ]
        )
    return [np.stack(t) for t in zip(*out)]


def class_table(mobility):
    plus, minus, _ = quadrature(mobility.shape[2])
    both = jnp.asarray(np.concatenate([plus, minus]), jnp.float32)
    value = MOBILE_BASE + jnp.einsum(
        "qk,mck->mqc", both, mobility, precision=lax.Precision.HIGHEST
    )
    parts = []
    for _ in range(3):
        part = lax.reduce_precision(value, 8, 7)
        parts.append(part)
        value = value - part
    eye = jnp.eye(TILE, dtype=jnp.float32)
    wide = [
        (p[:, :, None, :, None] * eye[None, None, :, None, :]).reshape(
            p.shape[0], p.shape[1] * TILE, p.shape[2] * TILE
        )
        for p in parts
    ]
    return jnp.concatenate(wide, axis=2).astype(jnp.bfloat16)


def split3(value):
    high = value.astype(jnp.bfloat16)
    low = (value - high.astype(jnp.float32)).astype(jnp.bfloat16)
    return jnp.concatenate([high, low, high], axis=0)


def dot(a, b):
    return jnp.dot(a, b, preferred_element_type=jnp.float32)


def couple(operated, material, classes, mats):
    fwd_e, fwd_o, back_e, back_o, ctab = mats
    hot = jnp.concatenate(
        [jnp.where(material == c, 1.0, 0.0) for c in range(classes)], axis=0
    ).astype(jnp.bfloat16)
    factor = dot(ctab[...], jnp.concatenate([hot, hot, hot], axis=0))
    even = dot(fwd_e[...], split3(jnp.concatenate(operated[0::2], axis=0)))
    odd = dot(fwd_o[...], split3(jnp.concatenate(operated[1::2], axis=0)))
    half = even.shape[0]
    up = factor[:half] * (even + odd)
    down = factor[half:] * (even - odd)
    parts = (dot(back_e[...], split3(up + down)), dot(back_o[...], split3(up - down)))
    return [
        parts[j % 2][TILE * (j // 2) : TILE * (j // 2 + 1)] for j in range(len(operated))
    ]


def step_kernel(
    n_blocks, n_out, sides, modes, classes, *refs
):
    refs = list(refs)

    def take(count):
        got = refs[:count]
        del refs[:count]
        return got

    blocks = take(n_blocks)
    xlo, xhi, up8, dn8 = take(4)
    vel, dis, mat, mov = take(4)
    mats = take(5)
    if sides:
        near, ysum, vel_e, dis_e, mat_e, mov_e = take(6)
    outs = take(n_out)
    if sides:
        (ext_out,) = take(1)
    scr, sems = take(2)
    planes, rows, nz = vel.shape
    copies = []
    width = modes // n_blocks
    for b, ref in enumerate(blocks):
        copies.append((ref, scr.at[pl.ds(b * width, width), pl.ds(2, planes), pl.ds(TILE, rows)]))
    copies.append((xlo, scr.at[:, pl.ds(0, 2), pl.ds(TILE, rows)]))
    copies.append((xhi, scr.at[:, pl.ds(planes + 2, 2), pl.ds(TILE, rows)]))
    copies.append((up8, scr.at[:, pl.ds(2, planes), pl.ds(0, TILE)]))
    copies.append((dn8, scr.at[:, pl.ds(2, planes), pl.ds(TILE + rows, TILE)]))
    started = [
        pltpu.make_async_copy(src, dst, sems.at[i]) for i, (src, dst) in enumerate(copies)
    ]
    for copy in started:
        copy.start()

    lane = lax.broadcasted_iota(jnp.int32, (TILE, nz), 1)
    first, final = lane == 0, lane == nz - 1

    def z_sum(centre):
        lower = jnp.where(first, 0.0, pltpu.roll(centre, 1, 1))
        upper = jnp.where(final, 0.0, pltpu.roll(centre, nz - 1, 1))
        return lower + upper

    def weights(v, d):
        return (
            d * (-1.0 / 12.0) - v * (1.0 / 6.0),
            d * (16.0 / 12.0) + v,
            d * -6.5 - v * 0.5,
            d * (16.0 / 12.0) - v * (1.0 / 3.0),
            d * (-1.0 / 12.0),
        )

    def operate(w, d, v5, ypair):
        total = d * (ypair + z_sum(v5[2]))
        for a, b in zip(w, v5):
            total = total + a * b
        return total

    if sides:
        for s in range(sides):
            for g in range(planes // TILE):
                at = slice(g * TILE, (g + 1) * TILE)
                d = dis_e[s, at]
                w = weights(vel_e[s, at], d)
                ops = []
                for j in range(modes):
                    v5 = [near[s, j, g * TILE + o : g * TILE + o + TILE] for o in range(5)]
                    ops.append(operate(w, d, v5, ysum[s, j, at]))
                coupled = couple(ops, mat_e[s, at], classes, mats)
                scale = mov_e[s, at]
                for j in range(modes):
                    ext_out[s, j, at] = (
                        near[s, j, g * TILE + 2 : g * TILE + 2 + TILE] + scale * coupled[j]
                    )
    for copy in started:
        copy.wait()

    y_tiles = rows // TILE

    def body(t, carry):
        x = t // y_tiles
        y0 = pl.multiple_of((t % y_tiles) * TILE, TILE)
        here = (x, pl.ds(y0, TILE))
        d = dis[here]
        w = weights(vel[here], d)
        inner = pl.ds(pl.multiple_of(y0 + TILE, TILE), TILE)
        ops = []
        for j in range(modes):
            tall = scr[j, x + 2, pl.ds(y0, 3 * TILE)]
            ypair = tall[TILE - 1 : 2 * TILE - 1] + tall[TILE + 1 : 2 * TILE + 1]
            v5 = [scr[j, x + o, inner] for o in range(5)]
            ops.append(operate(w, d, v5, ypair))
        coupled = couple(ops, mat[here], classes, mats)
        scale = mov[here]
        share = modes // n_out
        for j in range(modes):
            outs[j // share][j % share, x, pl.ds(y0, TILE)] = (
                scr[j, x + 2, inner] + scale * coupled[j]
            )
        return carry

    lax.fori_loop(0, planes * y_tiles, body, 0, unroll=2)


def run_step(blocks, xlo, xhi, up8, dn8, cells, mats, ext, n_out, classes):
    sides = ext[0].shape[0] if ext else 0
    modes = xlo.shape[0]
    planes, rows, nz = cells[0].shape
    any_spec = pl.BlockSpec(memory_space=pl.ANY)
    vmem = pl.BlockSpec(memory_space=pltpu.VMEM)
    operands = [*blocks, xlo, xhi, up8, dn8, *cells, *mats, *ext]
    n_any = len(blocks) + 4
    shapes = [jax.ShapeDtypeStruct((modes // n_out, planes, rows, nz), jnp.float32)] * n_out
    if sides:
        shapes = shapes + [jax.ShapeDtypeStruct((sides, modes, planes, nz), jnp.float32)]
    padded = modes * (planes + 4) * (rows + 2 * TILE) * nz
    return pl.pallas_call(
        functools.partial(step_kernel, len(blocks), n_out, sides, modes, classes),
        out_shape=shapes,
        in_specs=[any_spec] * n_any + [vmem] * (len(operands) - n_any),
        out_specs=[vmem] * len(shapes),
        scratch_shapes=[
            pltpu.VMEM((modes, planes + 4, rows + 2 * TILE, nz), jnp.float32),
            pltpu.SemaphoreType.DMA((n_any,)),
        ],
        compiler_params=pltpu.CompilerParams(vmem_limit_bytes=32 * 1024 * 1024),
        cost_estimate=pl.CostEstimate(
            flops=modes * planes * rows * nz * 2000, bytes_accessed=8 * padded, transcendentals=0
        ),
        name="step_first" if sides else "step_last",
    )(*operands)


def on_device(field, velocity, dispersion, mobility, material, fixed_mask):
    metals, width, planes, ny, nz = field.shape
    modes, classes = mobility.shape[2], mobility.shape[1]
    n = lax.axis_size("mode")
    q = lax.axis_index("mode")
    size = lax.axis_size("space")
    rows = ny // n
    up_perm = [(i, i + 1) for i in range(size - 1)]
    down_perm = [(i + 1, i) for i in range(size - 1)]
    movable = TIME_STEP * (1 - fixed_mask).astype(jnp.float32)

    def shift(d):
        return [(i, (i + d) % n) for i in range(n)]

    def block_rows(array, axis, owner):
        return lax.dynamic_slice_in_dim(array, owner * rows, rows, axis)

    def row(array, axis, index):
        return lax.dynamic_index_in_dim(array, jnp.clip(index, 0, ny - 1), axis, keepdims=False)

    def side_rows(owner):
        signs = [jnp.where(owner == 0, 1, -1)] if n == 2 else [1, -1]
        out = []
        for sign in signs:
            near = owner * rows + jnp.where(sign > 0, rows, -1)
            inside = jnp.where(sign > 0, rows - 1, 0)
            out.append((near, near + sign, inside, (near >= 0) & (near < ny)))
        return out

    def ext_rows(values, owner):
        return jnp.stack(
            [
                jnp.where(
                    valid, jnp.stack([row(values, 2, near), row(values, 2, far)]), 0.0
                )
                for near, far, _, valid in side_rows(owner)
            ]
        )

    def pick_sides(ext):
        if n == 2:
            above = jnp.where(q == 0, 0.0, ext[0])
            below = jnp.where(q == 0, ext[0], 0.0)
        else:
            below, above = ext[0], ext[1]
        above = jnp.pad(above[:, :, None], ((0, 0), (0, 0), (TILE - 1, 0), (0, 0)))
        below = jnp.pad(below[:, :, None], ((0, 0), (0, 0), (0, TILE - 1), (0, 0)))
        return above, below

    def beside(low, high):
        return lax.ppermute(high, "space", up_perm), lax.ppermute(low, "space", down_perm)

    cells = [block_rows(a, 1, q) for a in (velocity, dispersion, material, movable)]
    ext_cells = [
        jnp.stack([row(a, 1, near) for near, _, _, _ in side_rows(q)])
        for a in (velocity, dispersion, material)
    ]
    ext_cells.append(
        jnp.stack([jnp.where(ok, row(movable, 1, near), 0.0) for near, _, _, ok in side_rows(q)])
    )
    base = [
        lax.dynamic_index_in_dim(jnp.asarray(t), q, 0, keepdims=False)
        for t in tables(modes, n)
    ]
    ctabs = class_table(mobility)

    arrived = []
    for m in range(metals):
        exts, blocks = [ext_rows(field[m], q)], [block_rows(field[m], 2, q)]
        for d in range(1, n):
            target = lax.rem(q + d, n)
            exts.append(lax.ppermute(ext_rows(field[m], target), "mode", shift(d)))
            blocks.append(lax.ppermute(block_rows(field[m], 2, target), "mode", shift(d)))
        arrived.append((exts, blocks))

    result = jnp.zeros(field.shape, jnp.float32)
    for m in range(metals):
        exts, blocks = arrived[m]
        mats = base + [ctabs[m]]
        ext = jnp.concatenate(exts, axis=2)
        near, far = ext[:, 0], ext[:, 1]
        near_lo, near_hi = beside(near[:, :, :2], near[:, :, planes - 2 :])
        inside = jnp.stack(
            [
                jnp.concatenate(
                    [lax.dynamic_index_in_dim(b, at, 2, keepdims=False) for b in blocks], axis=0
                )
                for _, _, at, _ in side_rows(q)
            ]
        )
        xlo, xhi = beside(
            jnp.concatenate([b[:, :2] for b in blocks], axis=0),
            jnp.concatenate([b[:, planes - 2 :] for b in blocks], axis=0),
        )
        padded = jnp.concatenate([near_lo, near, near_hi], axis=2)
        state, ext_new = run_step(
            blocks, xlo, xhi, *pick_sides(near), cells, mats,
            [padded, far + inside, *ext_cells], 1, classes,
        )
        xlo, xhi = beside(state[:, :2], state[:, planes - 2 :])
        outs = run_step(
            [state], xlo, xhi, *pick_sides(ext_new), cells, mats, [], n, classes
        )
        zero = jnp.int32(0)
        for d in range(n):
            part = outs[d]
            if d:
                part = lax.ppermute(part, "mode", shift(n - d))
            owner = lax.rem(q + d, n)
            result = lax.dynamic_update_slice(
                result, part[None], (jnp.int32(m), zero, zero, owner * rows, zero)
            )
    return result


def solution(mesh):
    in_specs = (
        P(None, "mode", "space", None, None),
        P("space", None, None),
        P("space", None, None),
        P(),
        P("space", None, None),
        P("space", None, None),
    )
    out_specs = P(None, "mode", "space", None, None)
    return jax.shard_map(
        on_device, mesh=mesh, in_specs=in_specs, out_specs=out_specs, check_vma=False
    )
```

time: 975 us -> 467 us (0.48)
  matrix products: 306 us -> 0.15 us
  blocking collectives: 262 us -> 0 us
  other arithmetic: 119 us -> 10.7 us
  Pallas kernels: 0 us -> 94.2 us
  waiting for transfers between devices: 120 us -> 213 us
  local copies, waits for them, and re-layouts: 141 us -> 82.2 us
  starting transfers between devices: 18.9 us -> 62.9 us
    dot_general x17 -> x1, matrix products: 306 us -> 0.15 us  [class_table(): jnp.einsum('qk,mck->mqc', both, mobility, precision=lax.Precision.HIGHEST)]
    all_to_all x2 -> x0, blocking collectives: 262 us -> none  [the longest x1 152 us: on_device(): lax.all_to_all(field, 'mode', split_axis=3, concat_axis=1, tiled=True)]
    pallas_call x0 -> x6, Pallas kernels: none -> 94.2 us  [run_step(): pl.pallas_call(functools.partial(step_kernel, len(blocks), n_out, sides,...]
    ppermute x8 -> x27, waiting for transfers between devices: 120 us -> 213 us  [the longest x3 88.2 us: on_device(): exts.append(lax.ppermute(ext_rows(field[m], target), 'mode', shift(d)))]
    mul x4 -> x1, other arithmetic: 91.8 us -> 1.9 us  [on_device(): movable = TIME_STEP * (1 - fixed_mask).astype(jnp.float32)]
    while x5 -> x0, local copies, waits for them, and re-layouts: 81.4 us -> none  [class_terms(): return lax.fori_loop(0, class_mats.shape[1], add_class, total)]
    ppermute x8 -> x27, starting transfers between devices: 18.9 us -> 62.9 us  [the longest x9 30.9 us: beside(): lax.ppermute(low, 'space', down_perm)]
    all_to_all x2 -> x0, local copies, waits for them, and re-layouts: 28.8 us -> none  [the longest x1 16.6 us: on_device(): lax.all_to_all(field, 'mode', split_axis=3, concat_axis=1, tiled=True)]
  transfers between devices with their start and end apart: 8 -> 27, of which waited for: 6 -> 8; matrix products, arithmetic and copies ran while one was open for 1% -> 15% of each run, Pallas kernels for 0% -> 20%
where the time goes in v1:
time: 467 us; the launch traced here: 464 us
  waiting for transfers between devices  213 us (46%)
  Pallas kernels  94.2 us (20%)
  local copies, waits for them, and re-layouts  82.2 us (18%)
  starting transfers between devices  62.9 us (13%)
  other arithmetic  10.7 us (2%)
    pallas_call x6, Pallas kernels, run_step(): pl.pallas_call(functools.partial(step_kernel, len(blocks), n_out, sides,...  94.2 us
    ppermute x3, waiting for transfers between devices, on_device(): exts.append(lax.ppermute(ext_rows(field[m], target), 'mode', shift(d)))  88.2 us
    ppermute x3, waiting for transfers between devices, on_device(): part = lax.ppermute(part, 'mode', shift(n - d))  83.8 us
    ppermute x9, waiting for transfers between devices, beside(): lax.ppermute(low, 'space', down_perm)  38.4 us
    ppermute x9, starting transfers between devices, beside(): lax.ppermute(low, 'space', down_perm)  30.9 us
    ppermute x9, starting transfers between devices, beside(): lax.ppermute(high, 'space', up_perm)  22.4 us
    mul x12, local copies, waits for them, and re-layouts, class_table(): p[:, :, None, :, None] * eye[None, None, :, None, :]  18.3 us
    dynamic_slice x6, local copies, waits for them, and re-layouts, block_rows(): return lax.dynamic_slice_in_dim(array, owner * rows, rows, axis)  10.1 us
  transfers between devices with their start and end apart: 27, of which 8 were waited for; matrix products, arithmetic and copies ran while one was open for 15% of the time, Pallas kernels for 20%

profile of v1, /device:TPU:10, one launch (start us, length us, event | category | flops | bytes accessed | tf_op | source)
XLA Modules:
  0.0 464.4 jit_solution(5131797403010173594)
XLA Ops:
  0.0 9.9 %fusion.21 = (f32[1,8,8,64,256]{4,3,2,1,0:T(8,128)}, f32[1,8,8,64,256]{4,3,2,1,0:T(8,128)}, f32[1,8,8,64,256]{4,3,2,1,0:T(8,128)}) fusion(f32[3,8,8,64,256]{4,3,2,1,0:T(8,128)} %param.11), kind=kLoop, calls=%fused_computation.133 | loop fusion | bytes 25165824 | tf_op jit(solution)/shard_map/slice | solution.py:304
  9.9 4.1 constant_dynamic-slice_fusion.1
  14.6 1.5 collective-permute-start.21
  16.1 4.2 dynamic-slice_bitcast_fusion
  20.9 2.5 dynamic-slice_bitcast_fusion.2
  23.4 1.5 collective-permute-start.9
  26.1 2.3 dynamic-slice_bitcast_fusion.4
  28.4 1.5 collective-permute-start
  30.6 3.0 constant_dynamic-slice_fusion.17
  35.7 1.9 convert_multiply_fusion
  38.6 1.5 constant_dynamic-slice_fusion.14
  40.2 1.6 mul.102
  41.8 2.3 mul.103
  45.0 1.6 mul.108
  46.7 2.3 mul.109
  49.9 1.6 mul.111
  51.5 2.4 mul.112
  54.7 1.7 mul.104
  56.4 1.4 mul.105
  58.5 1.5 copy.132
  60.6 2.3 fusion.27
  68.4 1.4 multiply_convert_fusion.2
  72.0 44.9 %collective-permute-done.12 = f32[1,2,8,8,256]{4,3,2,1,0:T(8,128)} collective-permute-done((f32[1,2,8,8,256]{4,3,2,1,0:T(8,128)}, f32[1,2,8,8,256]{4,3,2,1,0:T(8,128)}, u32[]{:S(2)}, u32[]{:S(2)}) %collective-permute-start.12) | collective-permute-done | bytes 131104 | tf_op jit(solution)/shard_map/ppermute | solution.py:307
  116.9 1.9 collective-permute-start.22
  119.8 43.3 %collective-permute-done.3 = f32[1,2,8,8,256]{4,3,2,1,0:T(8,128)S(1)} collective-permute-done((f32[1,2,8,8,256]{4,3,2,1,0:T(8,128)S(1)}, f32[1,2,8,8,256]{4,3,2,1,0:T(8,128)S(1)}, u32[]{:S(2)}, u32[]{:S(2)}) %collective-permute-start.3) | collective-permute-done | bytes 131104 | tf_op jit(solution)/shard_map/ppermute | solution.py:307
  163.2 1.9 collective-permute-start.23
  166.8 2.4 collective-permute-start.13
  169.3 3.2 collective-permute-start.14
  172.5 1.9 collective-permute-start.4
  174.4 3.6 collective-permute-start.5
  178.1 1.5 collective-permute-done.5
  179.7 1.3 fusion.30
  181.2 3.8 collective-permute-start.2
  185.1 3.6 collective-permute-start.1
  188.7 1.3 fusion.28
  190.2 4.7 %collective-permute-start.10 = (f32[16,2,32,256]{3,2,1,0:T(8,128)S(1)}, f32[16,2,32,256]{3,2,1,0:T(8,128)S(1)}, u32[]{:S(2)}, u32[]{:S(2)}) collective-permute-start(f32[16,2,32,256]{3,2,1,0:T(8,128)S(1)} %pad_maximum_fusion.2), channel_id=1, source_target_pairs={{0,2},{2,4},{4,6},{6,8},{8,10},{10,12},{12,14},{14,16},{16,18},{18... | collective-permute-start | bytes 3145736 | tf_op jit(solution)/shard_map/ppermute | solution.py:286
  194.9 1.3 fusion.26
  196.3 1.3 constant_dynamic-slice_fusion
  198.2 2.1 collective-permute-start.19
  200.4 3.6 collective-permute-start.11
  205.3 36.8 %collective-permute-done.2.refs_3_ = f32[16,2,32,256]{3,2,1,0:T(8,128)S(1)} collective-permute-done((f32[16,2,32,256]{3,2,1,0:T(8,128)S(1)}, f32[16,2,32,256]{3,2,1,0:T(8,128)S(1)}, u32[]{:S(2)}, u32[]{:S(2)}) %collective-permute-start.2) | collective-permute-done | bytes 1048608 | tf_op jit(solution)/shard_map/ppermute | solution.py:286
  242.2 3.8 collective-permute-start.20
  246.0 15.3 %step_first.3 = (f32[16,8,32,256]{3,2,1,0:T(8,128)S(1)}, f32[1,16,8,256]{3,2,1,0:T(8,128)S(1)}) custom-call(f32[8,8,32,256]{3,2,1,0:T(8,128)S(1)} %copy-done.3, f32[8,8,32,256]{3,2,1,0:T(8,128)} %collective-permute-done.refs_1_, f32[16,2,32,256]{3,2,1,0:T(8,128)S(1)} %collective-permute-done.1.refs_2_, ...), custom_call_target="tpu_custom_call" | custom-call | flops 2097152000 | bytes 18874368 | tf_op jit(solution)/shard_map/step_first/pallas_call | solution.py:219
  262.6 1.9 collective-permute-start.6
  264.5 3.6 collective-permute-start.7
  269.1 15.3 %step_first.4 = (f32[16,8,32,256]{3,2,1,0:T(8,128)S(1)}, f32[1,16,8,256]{3,2,1,0:T(8,128)S(1)}) custom-call(f32[8,8,32,256]{3,2,1,0:T(8,128)S(1)} %copy-done.2, f32[8,8,32,256]{3,2,1,0:T(8,128)} %collective-permute-done.9.refs_1_, f32[16,2,32,256]{3,2,1,0:T(8,128)S(1)} %collective-permute-done.10.refs_2_, ...), custom_call_target="tpu_custom_call" | custom-call | flops 2097152000 | bytes 18874368 | tf_op jit(solution)/shard_map/step_first/pallas_call | solution.py:219
  284.6 1.9 collective-permute-start.15
  287.1 3.6 collective-permute-start.16
  293.0 15.3 %step_first.5 = (f32[16,8,32,256]{3,2,1,0:T(8,128)S(1)}, f32[1,16,8,256]{3,2,1,0:T(8,128)S(1)}) custom-call(f32[8,8,32,256]{3,2,1,0:T(8,128)S(1)} %get-tuple-element.40.refs_0_, f32[8,8,32,256]{3,2,1,0:T(8,128)} %collective-permute-done.18.refs_1_, f32[16,2,32,256]{3,2,1,0:T(8,128)S(1)} %collective-permute-done.19.refs_2_, f32[16,2,32,256]{3,2,1,0:T(8,128)S(1)} %copy-done.9, ...), custom_call_target="tpu_custom_call" | custom-call | flops 2097152000 | bytes 18874368 | tf_op jit(solution)/shard_map/step_first/pallas_call | solution.py:219
  308.3 16.4 %step_last.3 = (f32[8,8,32,256]{3,2,1,0:T(8,128)S(1)}, f32[8,8,32,256]{3,2,1,0:T(8,128)}) custom-call(f32[16,8,32,256]{3,2,1,0:T(8,128)S(1)} %get-tuple-element.17.refs_0_, f32[16,2,32,256]{3,2,1,0:T(8,128)S(1)} %collective-permute-done.6.refs_1_, f32[16,2,32,256]{3,2,1,0:T(8,128)} %collective-permute-done.7.refs_2_, f32[16,8,8,256]{3,2,1,0:T(8,128)S(1)} %pad.40.refs_3_, ...), custom_call_target="tpu_custom_call" | custom-call | flops 2097152000 | bytes 18874368 | tf_op jit(solution)/shard_map/step_last/pallas_call | solution.py:219
  325.5 1.9 collective-permute-start.24
  327.5 3.6 collective-permute-start.25
  331.7 16.4 %step_last.4 = (f32[8,8,32,256]{3,2,1,0:T(8,128)S(1)}, f32[8,8,32,256]{3,2,1,0:T(8,128)}) custom-call(f32[16,8,32,256]{3,2,1,0:T(8,128)S(1)} %get-tuple-element.21.refs_0_, f32[16,2,32,256]{3,2,1,0:T(8,128)S(1)} %collective-permute-done.15.refs_1_, f32[16,2,32,256]{3,2,1,0:T(8,128)} %collective-permute-done.16.refs_2_, f32[16,8,8,256]{3,2,1,0:T(8,128)S(1)} %pad.44.refs_3_, ...), custom_call_target="tpu_custom_call" | custom-call | flops 2097152000 | bytes 18874368 | tf_op jit(solution)/shard_map/step_last/pallas_call | solution.py:219
  348.1 1.6 collective-permute-start.17
  350.2 2.7 collective-permute-done.24.refs_1_
  352.9 15.6 %step_last.5 = (f32[8,8,32,256]{3,2,1,0:T(8,128)S(1)}, f32[8,8,32,256]{3,2,1,0:T(8,128)}) custom-call(f32[16,8,32,256]{3,2,1,0:T(8,128)S(1)} %get-tuple-element.25.refs_0_, f32[16,2,32,256]{3,2,1,0:T(8,128)S(1)} %collective-permute-done.24.refs_1_, f32[16,2,32,256]{3,2,1,0:T(8,128)S(1)} %collective-permute-done.25.refs_2_, ...), custom_call_target="tpu_custom_call" | custom-call | flops 2097152000 | bytes 18874368 | tf_op jit(solution)/shard_map/step_last/pallas_call | solution.py:219
  368.5 1.3 copy-done.6
  369.8 1.5 collective-permute-start.26
  371.3 1.6 broadcast_in_dim.70
  373.6 2.0 bitcast_dynamic-update-slice_fusion.4
  375.8 42.7 %collective-permute-done.17 = f32[8,8,32,256]{3,2,1,0:T(8,128)} collective-permute-done((f32[8,8,32,256]{3,2,1,0:T(8,128)}, f32[8,8,32,256]{3,2,1,0:T(8,128)}, u32[]{:S(2)}, u32[]{:S(2)}) %collective-permute-start.17) | collective-permute-done | bytes 2097184 | tf_op jit(solution)/shard_map/ppermute | solution.py:343
  418.5 1.8 bitcast_dynamic-update-slice_fusion.2
  420.6 40.7 %collective-permute-done.26 = f32[8,8,32,256]{3,2,1,0:T(8,128)} collective-permute-done((f32[8,8,32,256]{3,2,1,0:T(8,128)}, f32[8,8,32,256]{3,2,1,0:T(8,128)}, u32[]{:S(2)}, u32[]{:S(2)}) %collective-permute-start.26) | collective-permute-done | bytes 2097184 | tf_op jit(solution)/shard_map/ppermute | solution.py:343
  461.3 3.2 bitcast_dynamic-update-slice_fusion
  (171 shorter events, 31.0 us)
Async XLA Ops:
  0.0 29.9 %copy-start = (s32[8,64,256]{2,1,0:T(8,128)S(1)}, s32[8,64,256]{2,1,0:T(8,128)}, u32[]{:S(2)}) copy-start(s32[8,64,256]{2,1,0:T(8,128)} %param.15) | copy-start | bytes 1572868
  14.6 56.9 %collective-permute-start.21 = (f32[1,2,8,8,256]{4,3,2,1,0:T(8,128)}, f32[1,2,8,8,256]{4,3,2,1,0:T(8,128)S(1)}, u32[]{:S(2)}, u32[]{:S(2)}) collective-permute-start(f32[1,2,8,8,256]{4,3,2,1,0:T(8,128)} %maximum_select_fusion.5), channel_id=1, source_target_pairs={{0,1},{1,0},{2,3},{3,2},{4,5},{5,4},{6,7},{7,6},{8,9},{9,8},{10,11... | collective-permute-start | bytes 393224 | tf_op jit(solution)/shard_map/ppermute | solution.py:307
  16.1 4.8 %copy-start.11 = (f32[1,8,8,64,256]{4,3,2,1,0:T(8,128)S(1)}, f32[1,8,8,64,256]{4,3,2,1,0:T(8,128)}, u32[]{:S(2)}) copy-start(f32[1,8,8,64,256]{4,3,2,1,0:T(8,128)} %get-tuple-element.30) | copy-start | bytes 12582916
  20.4 174.5 %collective-permute-start.18 = (f32[8,8,32,256]{3,2,1,0:T(8,128)}, f32[8,8,32,256]{3,2,1,0:T(8,128)}, u32[]{:S(2)}, u32[]{:S(2)}) collective-permute-start(f32[8,8,32,256]{3,2,1,0:T(8,128)} %get-tuple-element.39), channel_id=1, source_target_pairs={{0,1},{1,0},{2,3},{3,2},{4,5},{5,4},{6,7},{7,6},{8,9},{9,8},{10,11... | collective-permute-start | bytes 6291464 | tf_op jit(solution)/shard_map/ppermute | solution.py:308
  20.9 5.2 %copy-start.10 = (f32[1,8,8,64,256]{4,3,2,1,0:T(8,128)S(1)}, f32[1,8,8,64,256]{4,3,2,1,0:T(8,128)}, u32[]{:S(2)}) copy-start(f32[1,8,8,64,256]{4,3,2,1,0:T(8,128)} %get-tuple-element.31) | copy-start | bytes 12582916
  23.4 165.3 %collective-permute-start.9 = (f32[8,8,32,256]{3,2,1,0:T(8,128)}, f32[8,8,32,256]{3,2,1,0:T(8,128)}, u32[]{:S(2)}, u32[]{:S(2)}) collective-permute-start(f32[8,8,32,256]{3,2,1,0:T(8,128)} %get-tuple-element.48), channel_id=1, source_target_pairs={{0,1},{1,0},{2,3},{3,2},{4,5},{5,4},{6,7},{7,6},{8,9},{9,8},{10,11... | collective-permute-start | bytes 6291464 | tf_op jit(solution)/shard_map/ppermute | solution.py:308
  25.5 91.4 %collective-permute-start.12 = (f32[1,2,8,8,256]{4,3,2,1,0:T(8,128)}, f32[1,2,8,8,256]{4,3,2,1,0:T(8,128)}, u32[]{:S(2)}, u32[]{:S(2)}) collective-permute-start(f32[1,2,8,8,256]{4,3,2,1,0:T(8,128)} %maximum_select_fusion.3), channel_id=1, source_target_pairs={{0,1},{1,0},{2,3},{3,2},{4,5},{5,4},{6,7},{7,6},{8,9},{9,8},{10,11... | collective-permute-start | bytes 393224 | tf_op jit(solution)/shard_map/ppermute | solution.py:307
  28.4 151.3 %collective-permute-start = (f32[8,8,32,256]{3,2,1,0:T(8,128)}, f32[8,8,32,256]{3,2,1,0:T(8,128)}, u32[]{:S(2)}, u32[]{:S(2)}) collective-permute-start(f32[8,8,32,256]{3,2,1,0:T(8,128)} %get-tuple-element.57), channel_id=1, source_target_pairs={{0,1},{1,0},{2,3},{3,2},{4,5},{5,4},{6,7},{7,6},{8,9},{9,8},{10,11... | collective-permute-start | bytes 6291464 | tf_op jit(solution)/shard_map/ppermute | solution.py:308
  30.0 10.1 %copy-start.28 = (f32[3,8,16]{2,1,0:T(8,128)S(1)}, f32[3,8,16]{2,1,0:T(8,128)}, u32[]{:S(2)}) copy-start(f32[3,8,16]{2,1,0:T(8,128)} %param.14) | copy-start | bytes 4612
  30.0 10.1 %copy-start.29 = (f32[24,16,1]{0,1,2:T(8,128)S(1)}, f32[24,16,1]{0,1,2:T(8,128)}, u32[]{:S(2)}) copy-start(f32[24,16,1]{0,1,2:T(8,128)} %constant.230) | copy-start | bytes 4612
  51.5 8.5 %copy-start.20 = (f32[1,8,8,1,256]{4,3,2,1,0:T(1,128)S(1)}, f32[1,8,8,1,256]{4,3,2,1,0:T(1,128)}, u32[]{:S(2)}) copy-start(f32[1,8,8,1,256]{4,3,2,1,0:T(1,128)} %get-tuple-element.101) | copy-start | bytes 196612
  54.7 8.3 %copy-start.27 = (bf16[2,64,288]{2,1,0:T(8,128)(2,1)S(1)}, bf16[2,64,288]{2,1,0:T(8,128)(2,1)}, u32[]{:S(2)}) copy-start(bf16[2,64,288]{2,1,0:T(8,128)(2,1)} %constant.198.clone) | copy-start | bytes 221188
  60.6 5.9 %copy-start.21 = (f32[1,8,8,1,256]{4,3,2,1,0:T(1,128)S(1)}, f32[1,8,8,1,256]{4,3,2,1,0:T(1,128)}, u32[]{:S(2)}) copy-start(f32[1,8,8,1,256]{4,3,2,1,0:T(1,128)} %get-tuple-element.55) | copy-start | bytes 196612
  63.0 7.0 %copy-start.3 = (f32[8,8,32,256]{3,2,1,0:T(8,128)S(1)}, f32[8,8,32,256]{3,2,1,0:T(8,128)}, u32[]{:S(2)}) copy-start(f32[8,8,32,256]{3,2,1,0:T(8,128)} %get-tuple-element.58.refs_0_) | copy-start | bytes 6291460
  68.3 1.7 copy-start.16
  68.3 1.8 copy-start.18
  68.4 2.4 copy-start.26
  68.4 2.4 copy-start.17
  68.4 3.0 copy-start.19
  68.4 3.0 copy-start.25
  71.5 91.7 %collective-permute-start.3 = (f32[1,2,8,8,256]{4,3,2,1,0:T(8,128)S(1)}, f32[1,2,8,8,256]{4,3,2,1,0:T(8,128)S(1)}, u32[]{:S(2)}, u32[]{:S(2)}) collective-permute-start(f32[1,2,8,8,256]{4,3,2,1,0:T(8,128)S(1)} %maximum_select_fusion.1), channel_id=1, source_target_pairs={{0,1},{1,0},{2,3},{3,2},{4,5},{5,4},{6,7},{7,6},{8,9},{9,8},{10,11... | collective-permute-start | bytes 393224 | tf_op jit(solution)/shard_map/ppermute | solution.py:307
  116.9 49.9 %collective-permute-start.22 = (f32[1,16,2,256]{3,2,1,0:T(2,128)S(1)}, f32[1,16,2,256]{3,2,1,0:T(2,128)S(1)}, u32[]{:S(2)}, u32[]{:S(2)}) collective-permute-start(f32[1,16,2,256]{3,2,1,0:T(2,128)S(1)} %get-tuple-element.85), channel_id=1, source_target_pairs={{0,2},{2,4},{4,6},{6,8},{8,10},{10,12},{12,14},{14,16},{16,18},{18... | collective-permute-start | bytes 98312 | tf_op jit(solution)/shard_map/ppermute | solution.py:286
  163.2 6.1 %collective-permute-start.23 = (f32[1,16,2,256]{3,2,1,0:T(2,128)S(1)}, f32[1,16,2,256]{3,2,1,0:T(2,128)S(1)}, u32[]{:S(2)}, u32[]{:S(2)}) collective-permute-start(f32[1,16,2,256]{3,2,1,0:T(2,128)S(1)} %get-tuple-element.86), channel_id=1, source_target_pairs={{2,0},{4,2},{6,4},{8,6},{10,8},{12,10},{14,12},{16,14},{18,16},{20... | collective-permute-start | bytes 98312 | tf_op jit(solution)/shard_map/ppermute | solution.py:286
  166.8 5.6 %collective-permute-start.13 = (f32[1,16,2,256]{3,2,1,0:T(2,128)S(1)}, f32[1,16,2,256]{3,2,1,0:T(2,128)S(1)}, u32[]{:S(2)}, u32[]{:S(2)}) collective-permute-start(f32[1,16,2,256]{3,2,1,0:T(2,128)S(1)} %get-tuple-element.89), channel_id=1, source_target_pairs={{0,2},{2,4},{4,6},{6,8},{8,10},{10,12},{12,14},{14,16},{16,18},{18... | collective-permute-start | bytes 98312 | tf_op jit(solution)/shard_map/ppermute | solution.py:286
  169.3 5.2 %collective-permute-start.14 = (f32[1,16,2,256]{3,2,1,0:T(2,128)S(1)}, f32[1,16,2,256]{3,2,1,0:T(2,128)S(1)}, u32[]{:S(2)}, u32[]{:S(2)}) collective-permute-start(f32[1,16,2,256]{3,2,1,0:T(2,128)S(1)} %get-tuple-element.90), channel_id=1, source_target_pairs={{2,0},{4,2},{6,4},{8,6},{10,8},{12,10},{14,12},{16,14},{18,16},{20... | collective-permute-start | bytes 98312 | tf_op jit(solution)/shard_map/ppermute | solution.py:286
  172.5 5.6 %collective-permute-start.4 = (f32[1,16,2,256]{3,2,1,0:T(2,128)S(1)}, f32[1,16,2,256]{3,2,1,0:T(2,128)S(1)}, u32[]{:S(2)}, u32[]{:S(2)}) collective-permute-start(f32[1,16,2,256]{3,2,1,0:T(2,128)S(1)} %get-tuple-element.93), channel_id=1, source_target_pairs={{0,2},{2,4},{4,6},{6,8},{8,10},{10,12},{12,14},{14,16},{16,18},{18... | collective-permute-start | bytes 98312 | tf_op jit(solution)/shard_map/ppermute | solution.py:286
  174.4 5.2 %collective-permute-start.5 = (f32[1,16,2,256]{3,2,1,0:T(2,128)S(1)}, f32[1,16,2,256]{3,2,1,0:T(2,128)S(1)}, u32[]{:S(2)}, u32[]{:S(2)}) collective-permute-start(f32[1,16,2,256]{3,2,1,0:T(2,128)S(1)} %get-tuple-element.94), channel_id=1, source_target_pairs={{2,0},{4,2},{6,4},{8,6},{10,8},{12,10},{14,12},{16,14},{18,16},{20... | collective-permute-start | bytes 98312 | tf_op jit(solution)/shard_map/ppermute | solution.py:286
  181.1 8.9 %copy-start.15 = (f32[8,2,32,256]{3,2,1,0:T(8,128)S(1)}, f32[8,2,32,256]{3,2,1,0:T(8,128)}, u32[]{:S(2)}) copy-start(f32[8,2,32,256]{3,2,1,0:T(8,128)} %get-tuple-element.64) | copy-start | bytes 1572868
  181.2 61.0 %collective-permute-start.2 = (f32[16,2,32,256]{3,2,1,0:T(8,128)S(1)}, f32[16,2,32,256]{3,2,1,0:T(8,128)S(1)}, u32[]{:S(2)}, u32[]{:S(2)}) collective-permute-start(f32[16,2,32,256]{3,2,1,0:T(8,128)S(1)} %pad_maximum_fusion.1), channel_id=1, source_target_pairs={{2,0},{4,2},{6,4},{8,6},{10,8},{12,10},{14,12},{16,14},{18,16},{20... | collective-permute-start | bytes 3145736 | tf_op jit(solution)/shard_map/ppermute | solution.py:286
  185.1 60.9 %collective-permute-start.1 = (f32[16,2,32,256]{3,2,1,0:T(8,128)S(1)}, f32[16,2,32,256]{3,2,1,0:T(8,128)S(1)}, u32[]{:S(2)}, u32[]{:S(2)}) collective-permute-start(f32[16,2,32,256]{3,2,1,0:T(8,128)S(1)} %pad_maximum_fusion), channel_id=1, source_target_pairs={{0,2},{2,4},{4,6},{6,8},{8,10},{10,12},{12,14},{14,16},{16,18},{18... | collective-permute-start | bytes 3145736 | tf_op jit(solution)/shard_map/ppermute | solution.py:286
  190.0 6.2 %copy-start.13 = (f32[8,2,32,256]{3,2,1,0:T(8,128)S(1)}, f32[8,2,32,256]{3,2,1,0:T(8,128)}, u32[]{:S(2)}) copy-start(f32[8,2,32,256]{3,2,1,0:T(8,128)} %get-tuple-element.60) | copy-start | bytes 1572868
  190.2 10.2 %copy-start.14 = (f32[8,2,32,256]{3,2,1,0:T(8,128)S(1)}, f32[8,2,32,256]{3,2,1,0:T(8,128)}, u32[]{:S(2)}) copy-start(f32[8,2,32,256]{3,2,1,0:T(8,128)} %get-tuple-element.63) | copy-start | bytes 1572868
  190.2 74.3 %collective-permute-start.10 = (f32[16,2,32,256]{3,2,1,0:T(8,128)S(1)}, f32[16,2,32,256]{3,2,1,0:T(8,128)S(1)}, u32[]{:S(2)}, u32[]{:S(2)}) collective-permute-start(f32[16,2,32,256]{3,2,1,0:T(8,128)S(1)} %pad_maximum_fusion.2), channel_id=1, source_target_pairs={{0,2},{2,4},{4,6},{6,8},{8,10},{10,12},{12,14},{14,16},{16,18},{18... | collective-permute-start | bytes 3145736 | tf_op jit(solution)/shard_map/ppermute | solution.py:286
  198.2 88.9 %collective-permute-start.19 = (f32[16,2,32,256]{3,2,1,0:T(8,128)S(1)}, f32[16,2,32,256]{3,2,1,0:T(8,128)S(1)}, u32[]{:S(2)}, u32[]{:S(2)}) collective-permute-start(f32[16,2,32,256]{3,2,1,0:T(8,128)S(1)} %pad_maximum_fusion.4), channel_id=1, source_target_pairs={{0,2},{2,4},{4,6},{6,8},{8,10},{10,12},{12,14},{14,16},{16,18},{18... | collective-permute-start | bytes 3145736 | tf_op jit(solution)/shard_map/ppermute | solution.py:286
  200.4 68.6 %collective-permute-start.11 = (f32[16,2,32,256]{3,2,1,0:T(8,128)S(1)}, f32[16,2,32,256]{3,2,1,0:T(8,128)S(1)}, u32[]{:S(2)}, u32[]{:S(2)}) collective-permute-start(f32[16,2,32,256]{3,2,1,0:T(8,128)S(1)} %pad_maximum_fusion.3), channel_id=1, source_target_pairs={{2,0},{4,2},{6,4},{8,6},{10,8},{12,10},{14,12},{16,14},{18,16},{20... | collective-permute-start | bytes 3145736 | tf_op jit(solution)/shard_map/ppermute | solution.py:286
  242.2 48.6 %collective-permute-start.20 = (f32[16,2,32,256]{3,2,1,0:T(8,128)S(1)}, f32[16,2,32,256]{3,2,1,0:T(8,128)S(1)}, u32[]{:S(2)}, u32[]{:S(2)}) collective-permute-start(f32[16,2,32,256]{3,2,1,0:T(8,128)S(1)} %pad_maximum_fusion.5), channel_id=1, source_target_pairs={{2,0},{4,2},{6,4},{8,6},{10,8},{12,10},{14,12},{16,14},{18,16},{20... | collective-permute-start | bytes 3145736 | tf_op jit(solution)/shard_map/ppermute | solution.py:286
  261.3 6.8 %copy-start.22 = (f32[1,8,8,1,256]{4,2,1,3,0:T(8,128)S(1)}, f32[1,8,8,1,256]{4,2,1,3,0:T(8,128)}, u32[]{:S(2)}) copy-start(f32[1,8,8,1,256]{4,2,1,3,0:T(8,128)} %copy.124) | copy-start | bytes 196612
  261.3 6.8 %copy-start.24 = (f32[8,8,1,256]{3,1,2,0:T(8,128)S(1)}, f32[8,8,1,256]{3,1,2,0:T(8,128)}, u32[]{:S(2)}) copy-start(f32[8,8,1,256]{3,1,2,0:T(8,128)} %copy.135) | copy-start | bytes 196612
  261.3 6.9 %copy-start.23 = (f32[1,8,8,1,256]{4,2,1,3,0:T(8,128)S(1)}, f32[1,8,8,1,256]{4,2,1,3,0:T(8,128)}, u32[]{:S(2)}) copy-start(f32[1,8,8,1,256]{4,2,1,3,0:T(8,128)} %copy.129) | copy-start | bytes 196612
  261.3 7.8 %copy-start.2 = (f32[8,8,32,256]{3,2,1,0:T(8,128)S(1)}, f32[8,8,32,256]{3,2,1,0:T(8,128)}, u32[]{:S(2)}) copy-start(f32[8,8,32,256]{3,2,1,0:T(8,128)} %get-tuple-element.49.refs_0_) | copy-start | bytes 6291460
  262.6 45.7 %collective-permute-start.6 = (f32[16,2,32,256]{3,2,1,0:T(8,128)}, f32[16,2,32,256]{3,2,1,0:T(8,128)S(1)}, u32[]{:S(2)}, u32[]{:S(2)}) collective-permute-start(f32[16,2,32,256]{3,2,1,0:T(8,128)} %get-tuple-element.51), channel_id=1, source_target_pairs={{0,2},{2,4},{4,6},{6,8},{8,10},{10,12},{12,14},{14,16},{16,18},{18... | collective-permute-start | bytes 3145736 | tf_op jit(solution)/shard_map/ppermute | solution.py:286
  264.5 43.8 %collective-permute-start.7 = (f32[16,2,32,256]{3,2,1,0:T(8,128)S(1)}, f32[16,2,32,256]{3,2,1,0:T(8,128)}, u32[]{:S(2)}, u32[]{:S(2)}) collective-permute-start(f32[16,2,32,256]{3,2,1,0:T(8,128)S(1)} %get-tuple-element.50), channel_id=1, source_target_pairs={{2,0},{4,2},{6,4},{8,6},{10,8},{12,10},{14,12},{16,14},{18,16},{20... | collective-permute-start | bytes 3145736 | tf_op jit(solution)/shard_map/ppermute | solution.py:286
  284.6 47.0 %collective-permute-start.15 = (f32[16,2,32,256]{3,2,1,0:T(8,128)S(1)}, f32[16,2,32,256]{3,2,1,0:T(8,128)S(1)}, u32[]{:S(2)}, u32[]{:S(2)}) collective-permute-start(f32[16,2,32,256]{3,2,1,0:T(8,128)S(1)} %get-tuple-element.42), channel_id=1, source_target_pairs={{0,2},{2,4},{4,6},{6,8},{8,10},{10,12},{12,14},{14,16},{16,18},{18... | collective-permute-start | bytes 3145736 | tf_op jit(solution)/shard_map/ppermute | solution.py:286
  287.1 44.6 %collective-permute-start.16 = (f32[16,2,32,256]{3,2,1,0:T(8,128)S(1)}, f32[16,2,32,256]{3,2,1,0:T(8,128)}, u32[]{:S(2)}, u32[]{:S(2)}) collective-permute-start(f32[16,2,32,256]{3,2,1,0:T(8,128)S(1)} %get-tuple-element.41), channel_id=1, source_target_pairs={{2,0},{4,2},{6,4},{8,6},{10,8},{12,10},{14,12},{16,14},{18,16},{20... | collective-permute-start | bytes 3145736 | tf_op jit(solution)/shard_map/ppermute | solution.py:286
  290.8 1.0 copy-start.8
  291.8 1.2 copy-start.9
  324.7 48.9 %collective-permute-start.8 = (f32[8,8,32,256]{3,2,1,0:T(8,128)}, f32[8,8,32,256]{3,2,1,0:T(8,128)}, u32[]{:S(2)}, u32[]{:S(2)}) collective-permute-start(f32[8,8,32,256]{3,2,1,0:T(8,128)} %get-tuple-element.20), channel_id=1, source_target_pairs={{0,1},{1,0},{2,3},{3,2},{4,5},{5,4},{6,7},{7,6},{8,9},{9,8},{10,11... | collective-permute-start | bytes 6291464 | tf_op jit(solution)/shard_map/ppermute | solution.py:343
  325.5 27.4 %collective-permute-start.24 = (f32[16,2,32,256]{3,2,1,0:T(8,128)S(1)}, f32[16,2,32,256]{3,2,1,0:T(8,128)S(1)}, u32[]{:S(2)}, u32[]{:S(2)}) collective-permute-start(f32[16,2,32,256]{3,2,1,0:T(8,128)S(1)} %get-tuple-element.33), channel_id=1, source_target_pairs={{0,2},{2,4},{4,6},{6,8},{8,10},{10,12},{12,14},{14,16},{16,18},{18... | collective-permute-start | bytes 3145736 | tf_op jit(solution)/shard_map/ppermute | solution.py:286
  327.5 25.4 %collective-permute-start.25 = (f32[16,2,32,256]{3,2,1,0:T(8,128)S(1)}, f32[16,2,32,256]{3,2,1,0:T(8,128)S(1)}, u32[]{:S(2)}, u32[]{:S(2)}) collective-permute-start(f32[16,2,32,256]{3,2,1,0:T(8,128)S(1)} %get-tuple-element.32), channel_id=1, source_target_pairs={{2,0},{4,2},{6,4},{8,6},{10,8},{12,10},{14,12},{16,14},{18,16},{20... | collective-permute-start | bytes 3145736 | tf_op jit(solution)/shard_map/ppermute | solution.py:286
  348.1 20.4 %copy-start.4 = (f32[8,8,32,256]{3,2,1,0:T(8,128)}, f32[8,8,32,256]{3,2,1,0:T(8,128)S(1)}, u32[]{:S(2)}) copy-start(f32[8,8,32,256]{3,2,1,0:T(8,128)S(1)} %get-tuple-element.23) | copy-start | bytes 6291460
  348.1 70.4 %collective-permute-start.17 = (f32[8,8,32,256]{3,2,1,0:T(8,128)}, f32[8,8,32,256]{3,2,1,0:T(8,128)}, u32[]{:S(2)}, u32[]{:S(2)}) collective-permute-start(f32[8,8,32,256]{3,2,1,0:T(8,128)} %get-tuple-element.24), channel_id=1, source_target_pairs={{0,1},{1,0},{2,3},{3,2},{4,5},{5,4},{6,7},{7,6},{8,9},{9,8},{10,11... | collective-permute-start | bytes 6291464 | tf_op jit(solution)/shard_map/ppermute | solution.py:343
  368.5 1.3 copy-start.6
  369.8 91.4 %collective-permute-start.26 = (f32[8,8,32,256]{3,2,1,0:T(8,128)}, f32[8,8,32,256]{3,2,1,0:T(8,128)}, u32[]{:S(2)}, u32[]{:S(2)}) collective-permute-start(f32[8,8,32,256]{3,2,1,0:T(8,128)} %get-tuple-element.28), channel_id=1, source_target_pairs={{0,1},{1,0},{2,3},{3,2},{4,5},{5,4},{6,7},{7,6},{8,9},{9,8},{10,11... | collective-permute-start | bytes 6291464 | tf_op jit(solution)/shard_map/ppermute | solution.py:343
  373.1 2.5 copy-start.5
  375.8 44.5 %copy-start.7 = (f32[8,8,32,256]{3,2,1,0:T(8,128)S(1)}, f32[8,8,32,256]{3,2,1,0:T(8,128)}, u32[]{:S(2)}) copy-start(f32[8,8,32,256]{3,2,1,0:T(8,128)} %copy-done.6) | copy-start | bytes 6291460
  420.4 44.1 %copy-start.1 = (s32[8,64,256]{2,1,0:T(8,128)S(1)}, s32[8,64,256]{2,1,0:T(8,128)}, u32[]{:S(2)}) copy-start(s32[8,64,256]{2,1,0:T(8,128)} %param.15) | copy-start | bytes 1572868
  420.6 40.7 %copy-start.12 = (f32[3,8,8,64,256]{4,3,2,1,0:T(8,128)}, f32[3,8,8,64,256]{4,3,2,1,0:T(8,128)S(1)}, u32[]{:S(2)}) copy-start(f32[3,8,8,64,256]{4,3,2,1,0:T(8,128)S(1)} %bitcast_dynamic-update-slice_fusion.1) | copy-start | bytes 37748740

commit v2 on v1

--- a/solution.py
+++ b/solution.py
@@ -8,7 +8,7 @@
 from jax.experimental.pallas import tpu as pltpu
 from jax.sharding import PartitionSpec as P
 
-STEPS = 2
+
 TIME_STEP = 0.1
 MOBILE_BASE = 0.7
 TILE = 8
@@ -262,15 +262,21 @@
             out.append((near, near + sign, inside, (near >= 0) & (near < ny)))
         return out
 
-    def ext_rows(values, owner):
+    def ext_rows(owner):
         return jnp.stack(
             [
-                jnp.where(
-                    valid, jnp.stack([row(values, 2, near), row(values, 2, far)]), 0.0
-                )
+                jnp.where(valid, jnp.stack([row(field, 3, near), row(field, 3, far)]), 0.0)
                 for near, far, _, valid in side_rows(owner)
             ]
         )
+
+    def field_block(m, owner):
+        zero = jnp.int32(0)
+        return lax.dynamic_slice(
+            field,
+            (jnp.int32(m), zero, zero, owner * rows, zero),
+            (1, width, planes, rows, nz),
+        )[0]
 
     def pick_sides(ext):
         if n == 2:
@@ -283,7 +289,18 @@
         return above, below
 
     def beside(low, high):
-        return lax.ppermute(high, "space", up_perm), lax.ppermute(low, "space", down_perm)
+        before = lax.ppermute(high, "space", up_perm)
+        after = lax.ppermute(low, "space", down_perm)
+        return before, after
+
+    exts = [lax.ppermute(ext_rows(lax.rem(q + d, n)), "mode", shift(d)) for d in range(1, n)]
+    arrived = []
+    for m in range(metals):
+        blocks = []
+        for d in range(1, n):
+            piece = field_block(m, lax.rem(q + d, n))
+            blocks.append(lax.ppermute(piece, "mode", shift(d)))
+        arrived.append([field_block(m, q)] + blocks)
 
     cells = [block_rows(a, 1, q) for a in (velocity, dispersion, material, movable)]
     ext_cells = [
@@ -299,44 +316,17 @@
     ]
     ctabs = class_table(mobility)
 
-    arrived = []
-    for m in range(metals):
-        exts, blocks = [ext_rows(field[m], q)], [block_rows(field[m], 2, q)]
-        for d in range(1, n):
-            target = lax.rem(q + d, n)
-            exts.append(lax.ppermute(ext_rows(field[m], target), "mode", shift(d)))
-            blocks.append(lax.ppermute(block_rows(field[m], 2, target), "mode", shift(d)))
-        arrived.append((exts, blocks))
-
-    result = jnp.zeros(field.shape, jnp.float32)
-    for m in range(metals):
-        exts, blocks = arrived[m]
-        mats = base + [ctabs[m]]
-        ext = jnp.concatenate(exts, axis=2)
-        near, far = ext[:, 0], ext[:, 1]
-        near_lo, near_hi = beside(near[:, :, :2], near[:, :, planes - 2 :])
-        inside = jnp.stack(
-            [
-                jnp.concatenate(
-                    [lax.dynamic_index_in_dim(b, at, 2, keepdims=False) for b in blocks], axis=0
-                )
-                for _, _, at, _ in side_rows(q)
-            ]
-        )
-        xlo, xhi = beside(
-            jnp.concatenate([b[:, :2] for b in blocks], axis=0),
-            jnp.concatenate([b[:, planes - 2 :] for b in blocks], axis=0),
-        )
-        padded = jnp.concatenate([near_lo, near, near_hi], axis=2)
-        state, ext_new = run_step(
-            blocks, xlo, xhi, *pick_sides(near), cells, mats,
-            [padded, far + inside, *ext_cells], 1, classes,
-        )
-        xlo, xhi = beside(state[:, :2], state[:, planes - 2 :])
+    ext = jnp.concatenate([ext_rows(q)] + exts, axis=3)
+    near_all, far_all = ext[:, 0], ext[:, 1]
+    near_lo, near_hi = beside(near_all[:, :, :, :2], near_all[:, :, :, planes - 2 :])
+    padded_all = jnp.concatenate([near_lo, near_all, near_hi], axis=3)
+
+    zero = jnp.int32(0)
+
+    def finish(m, result, state, again, ext_new):
         outs = run_step(
-            [state], xlo, xhi, *pick_sides(ext_new), cells, mats, [], n, classes
-        )
-        zero = jnp.int32(0)
+            [state], *again, *pick_sides(ext_new), cells, base + [ctabs[m]], [], n, classes
+        )
         for d in range(n):
             part = outs[d]
             if d:
@@ -345,6 +335,39 @@
             result = lax.dynamic_update_slice(
                 result, part[None], (jnp.int32(m), zero, zero, owner * rows, zero)
             )
+        return result
+
+    result = jnp.zeros(field.shape, jnp.float32)
+    for m in range(metals):
+        blocks = arrived[m]
+        if not m:
+            blocks, padded_all = lax.optimization_barrier((blocks, padded_all))
+        else:
+            blocks, ext_new = lax.optimization_barrier((blocks, ext_new))
+            pending = (state, again, ext_new)
+        mats = base + [ctabs[m]]
+        near, far = near_all[:, m], far_all[:, m]
+        inside = jnp.stack(
+            [
+                jnp.concatenate(
+                    [lax.dynamic_index_in_dim(b, at, 2, keepdims=False) for b in blocks], axis=0
+                )
+                for _, _, at, _ in side_rows(q)
+            ]
+        )
+        xlo, xhi = beside(
+            jnp.concatenate([b[:, :2] for b in blocks], axis=0),
+            jnp.concatenate([b[:, planes - 2 :] for b in blocks], axis=0),
+        )
+        if m:
+            result = finish(m - 1, result, *pending)
+        sides = pick_sides(near)
+        state, ext_new = run_step(
+            blocks, xlo, xhi, *sides, cells, mats,
+            [padded_all[:, m], far + inside, *ext_cells], 1, classes,
+        )
+        again = beside(state[:, :2], state[:, planes - 2 :])
+    result = finish(metals - 1, result, state, again, ext_new)
     return result
 
 
@@ -358,6 +381,8 @@
         P("space", None, None),
     )
     out_specs = P(None, "mode", "space", None, None)
+
+
     return jax.shard_map(
         on_device, mesh=mesh, in_specs=in_specs, out_specs=out_specs, check_vma=False
     )

time: 467 us -> 433 us (0.927)
  starting transfers between devices: 62.9 us -> 41 us
  local copies, waits for them, and re-layouts: 82.2 us -> 63 us
  waiting for transfers between devices: 213 us -> 225 us
    ppermute x27 -> x21, starting transfers between devices: 62.9 us -> 41 us  [the longest x7 20.5 us: beside(): after = lax.ppermute(low, 'space', down_perm)]
    ppermute x27 -> x21, waiting for transfers between devices: 213 us -> 225 us  [the longest x3 101 us: on_device(): blocks.append(lax.ppermute(piece, 'mode', shift(d)))]
    slice x7 -> x4, local copies, waits for them, and re-layouts: 11.6 us -> 0.78 us  [the longest x3 0.71 us: on_device(): again = beside(state[:, :2], state[:, planes - 2:])]
    squeeze x0 -> x2, local copies, waits for them, and re-layouts: none -> 9.65 us  [the longest x1 9.6 us: field_block(): lax.dynamic_slice(field, (jnp.int32(m), zero, zero, owner * rows, zero),...]
    dynamic_slice x6 -> x3, local copies, waits for them, and re-layouts: 10.1 us -> 1.17 us  [block_rows(): return lax.dynamic_slice_in_dim(array, owner * rows, rows, axis)]
    dynamic_slice x4 -> x6, local copies, waits for them, and re-layouts: 9.44 us -> 3.5 us  [on_device(): lax.dynamic_index_in_dim(b, at, 2, keepdims=False)]
    unnamed x83 -> x63, local copies, waits for them, and re-layouts: 9.77 us -> 8.77 us
  transfers between devices with their start and end apart: 27 -> 21, of which waited for: 8 -> 9; matrix products, arithmetic and copies ran while one was open for 15% -> 12% of each run, Pallas kernels for 20% -> 22%
where the time goes in v2:
time: 433 us; the launch traced here: 431 us
  waiting for transfers between devices  225 us (52%)
  Pallas kernels  93.9 us (22%)
  local copies, waits for them, and re-layouts  63 us (15%)
  starting transfers between devices  41 us (9%)
  other arithmetic  6.71 us (2%)
    ppermute x3, waiting for transfers between devices, on_device(): blocks.append(lax.ppermute(piece, 'mode', shift(d)))  101 us
    pallas_call x6, Pallas kernels, run_step(): pl.pallas_call(functools.partial(step_kernel, len(blocks), n_out, sides,...  93.9 us
    ppermute x3, waiting for transfers between devices, finish(): part = lax.ppermute(part, 'mode', shift(n - d))  65.4 us
    ppermute x7, waiting for transfers between devices, beside(): before = lax.ppermute(high, 'space', up_perm)  54.9 us
    ppermute x7, starting transfers between devices, beside(): after = lax.ppermute(low, 'space', down_perm)  20.5 us
    mul x12, local copies, waits for them, and re-layouts, class_table(): p[:, :, None, :, None] * eye[None, None, :, None, :]  17.6 us
    ppermute x7, starting transfers between devices, beside(): before = lax.ppermute(high, 'space', up_perm)  14.9 us
    squeeze x1, local copies, waits for them, and re-layouts, field_block(): lax.dynamic_slice(field, (jnp.int32(m), zero, zero, owner * rows, zero),...  9.6 us
  transfers between devices with their start and end apart: 21, of which 9 were waited for; matrix products, arithmetic and copies ran while one was open for 12% of the time, Pallas kernels for 22%

profile of v2, /device:TPU:10, one launch (start us, length us, event | category | flops | bytes accessed | tf_op | source)
XLA Modules:
  0.0 431.2 jit_solution(16314727026112126021)
XLA Ops:
  0.0 4.5 %constant_dynamic-slice_fusion.15 = (f32[3,8,8,1,256]{4,3,2,1,0:T(1,128)S(1)}, f32[3,8,8,1,256]{4,3,2,1,0:T(1,128)}, f32[3,8,8,1,256]{4,3,2,1,0:T(1,128)}, f32[3,8,8,1,256]{4,3,2,1,0:T(1,128)S(1)}) fusion(f32[3,8,8,64,256]{4,3,2,1,0:T(8,128)} %param.11, s32[]{:T(128)S(6)} %min.19, s32[]{:T(128)S(6)} %min.18, s32[]{:T(128)S(6)} %min.17, s32[]{:T(128)S(6)} %min.20), kind=kLoop, calls=%fused_computation.95 | loop fusion | bytes 1572880 | tf_op jit(solution)/shard_map/jit(dynamic_index_in_dim)/dynamic_slice | solution.py:254
  5.3 1.5 collective-permute-start.1
  6.9 9.6 %dynamic-slice_bitcast_fusion = (f32[8,8,32,256]{3,2,1,0:T(8,128)}, f32[8,8,32,256]{3,2,1,0:T(8,128)}, f32[8,8,32,256]{3,2,1,0:T(8,128)}, f32[8,8,32,256]{3,2,1,...) fusion(f32[3,8,8,64,256]{4,3,2,1,0:T(8,128)} %param.11, s32[]{:T(128)S(6)} %select_n.301, ...), kind=kLoop, calls=%fused_computation.6 | loop fusion | bytes 25165832 | tf_op jit(solution)/shard_map/squeeze | solution.py:275
  17.0 1.5 collective-permute-start.8
  19.1 0.9 constant_dynamic-slice_fusion.6
  20.2 0.9 mul.100
  21.1 1.4 mul.101
  23.2 1.6 mul.98
  24.8 2.3 mul.99
  27.3 1.6 mul.107
  28.9 2.3 mul.108
  31.4 1.6 mul.104
  33.1 3.0 mul.105
  36.0 1.8 copy.36
  37.8 1.2 multiply_convert_fusion.2
  39.0 0.9 pad_maximum_fusion.8
  39.9 0.8 maximum_select_fusion
  41.6 1.1 constant_dynamic-slice_fusion.10
  42.7 1.2 slice_bitcast_fusion.6
  43.9 1.3 fusion.3
  45.3 1.9 collective-permute-start.2
  47.2 3.6 collective-permute-start.3
  51.2 1.8 collective-permute-done.3
  53.2 100.5 %collective-permute-done.refs_1_ = f32[8,8,32,256]{3,2,1,0:T(8,128)} collective-permute-done((f32[8,8,32,256]{3,2,1,0:T(8,128)}, f32[8,8,32,256]{3,2,1,0:T(8,128)}, u32[]{:S(2)}, u32[]{:S(2)}) %collective-permute-start) | collective-permute-done | bytes 2097184 | tf_op jit(solution)/shard_map/ppermute | solution.py:302
  153.9 1.3 fusion.23
  155.3 1.9 collective-permute-start.4
  157.4 3.6 collective-permute-start.5
  161.8 1.1 constant_dynamic-slice_fusion.8
  163.0 19.7 %collective-permute-done.4.refs_2_ = f32[16,2,32,256]{3,2,1,0:T(8,128)S(1)} collective-permute-done((f32[16,2,32,256]{3,2,1,0:T(8,128)S(1)}, f32[16,2,32,256]{3,2,1,0:T(8,128)S(1)}, u32[]{:S(2)}, u32[]{:S(2)}) %collective-permute-start.4) | collective-permute-done | bytes 1048608 | tf_op jit(solution)/shard_map/ppermute | solution.py:292
  182.7 15.4 %step_first.3 = (f32[16,8,32,256]{3,2,1,0:T(8,128)S(1)}, f32[1,16,8,256]{3,2,1,0:T(8,128)S(1)}) custom-call(f32[8,8,32,256]{3,2,1,0:T(8,128)S(1)} %copy-done.3, f32[8,8,32,256]{3,2,1,0:T(8,128)} %collective-permute-done.refs_1_, f32[16,2,32,256]{3,2,1,0:T(8,128)S(1)} %collective-permute-done.4.refs_2_, ...), custom_call_target="tpu_custom_call" | custom-call | flops 2097152000 | bytes 18874368 | tf_op jit(solution)/shard_map/step_first/pallas_call | solution.py:219
  198.2 1.3 fusion.21
  199.7 1.9 collective-permute-start.10
  201.7 3.8 collective-permute-start.11
  206.7 1.1 constant_dynamic-slice_fusion.2
  208.1 1.9 collective-permute-start.7
  210.0 2.4 collective-permute-start.6
  212.4 25.8 %collective-permute-done.10.refs_2_ = f32[16,2,32,256]{3,2,1,0:T(8,128)S(1)} collective-permute-done((f32[16,2,32,256]{3,2,1,0:T(8,128)S(1)}, f32[16,2,32,256]{3,2,1,0:T(8,128)S(1)}, u32[]{:S(2)}, u32[]{:S(2)}) %collective-permute-start.10) | collective-permute-done | bytes 1048608 | tf_op jit(solution)/shard_map/ppermute | solution.py:292
  238.2 15.3 %step_first.4 = (f32[16,8,32,256]{3,2,1,0:T(8,128)S(1)}, f32[1,16,8,256]{3,2,1,0:T(8,128)S(1)}) custom-call(f32[8,8,32,256]{3,2,1,0:T(8,128)S(1)} %copy-done.2, f32[8,8,32,256]{3,2,1,0:T(8,128)} %collective-permute-done.8.refs_1_, f32[16,2,32,256]{3,2,1,0:T(8,128)S(1)} %collective-permute-done.10.refs_2_, ...), custom_call_target="tpu_custom_call" | custom-call | flops 2097152000 | bytes 18874368 | tf_op jit(solution)/shard_map/step_first/pallas_call | solution.py:219
  253.6 1.3 fusion.19
  255.1 1.9 collective-permute-start.16
  257.1 3.6 collective-permute-start.17
  261.4 1.1 constant_dynamic-slice_fusion
  262.8 1.9 collective-permute-start.13
  264.7 2.4 collective-permute-start.12
  267.1 15.6 %step_last.3 = (f32[8,8,32,256]{3,2,1,0:T(8,128)S(1)}, f32[8,8,32,256]{3,2,1,0:T(8,128)}) custom-call(f32[16,8,32,256]{3,2,1,0:T(8,128)S(1)} %get-tuple-element.29.refs_0_, f32[16,2,32,256]{3,2,1,0:T(8,128)S(1)} %collective-permute-done.6.refs_1_, f32[16,2,32,256]{3,2,1,0:T(8,128)S(1)} %collective-permute-done.7.refs_2_, f32[16,8,8,256]{3,2,1,0:T(8,128)S(1)} %pad.40.refs_3_, ...), custom_call_target="tpu_custom_call" | custom-call | flops 2097152000 | bytes 18874368 | tf_op jit(solution)/shard_map/step_last/pallas_call | solution.py:219
  282.7 1.4 copy-done.4
  284.6 9.1 %collective-permute-done.16.refs_2_ = f32[16,2,32,256]{3,2,1,0:T(8,128)S(1)} collective-permute-done((f32[16,2,32,256]{3,2,1,0:T(8,128)S(1)}, f32[16,2,32,256]{3,2,1,0:T(8,128)S(1)}, u32[]{:S(2)}, u32[]{:S(2)}) %collective-permute-start.16) | collective-permute-done | bytes 1048608 | tf_op jit(solution)/shard_map/ppermute | solution.py:292
  293.7 1.0 copy-done.8
  294.6 1.0 copy-done.10
  295.6 1.2 copy-done.9
  296.8 1.2 copy-done.11
  298.1 15.3 %step_first.5 = (f32[16,8,32,256]{3,2,1,0:T(8,128)S(1)}, f32[1,16,8,256]{3,2,1,0:T(8,128)S(1)}) custom-call(f32[8,8,32,256]{3,2,1,0:T(8,128)S(1)} %get-tuple-element.41.refs_0_, f32[8,8,32,256]{3,2,1,0:T(8,128)} %collective-permute-done.14.refs_1_, f32[16,2,32,256]{3,2,1,0:T(8,128)S(1)} %copy-done.9, f32[16,2,32,256]{3,2,1,0:T(8,128)S(1)} %copy-done.11, ...), custom_call_target="tpu_custom_call" | custom-call | flops 2097152000 | bytes 18874368 | tf_op jit(solution)/shard_map/step_first/pallas_call | solution.py:219
  313.6 1.9 collective-permute-start.19
  315.5 2.4 collective-permute-start.18
  318.5 16.6 %step_last.4 = (f32[8,8,32,256]{3,2,1,0:T(8,128)S(1)}, f32[8,8,32,256]{3,2,1,0:T(8,128)}) custom-call(f32[16,8,32,256]{3,2,1,0:T(8,128)S(1)} %get-tuple-element.36.refs_0_, f32[16,2,32,256]{3,2,1,0:T(8,128)} %collective-permute-done.12.refs_1_, f32[16,2,32,256]{3,2,1,0:T(8,128)} %collective-permute-done.13.refs_2_, f32[16,8,8,256]{3,2,1,0:T(8,128)S(1)} %pad.44.refs_3_, ...), custom_call_target="tpu_custom_call" | custom-call | flops 2097152000 | bytes 18874368 | tf_op jit(solution)/shard_map/step_last/pallas_call | solution.py:219
  336.2 2.8 collective-permute-done.19.refs_2_
  339.0 15.7 %step_last.5 = (f32[8,8,32,256]{3,2,1,0:T(8,128)S(1)}, f32[8,8,32,256]{3,2,1,0:T(8,128)}) custom-call(f32[16,8,32,256]{3,2,1,0:T(8,128)S(1)} %get-tuple-element.43.refs_0_, f32[16,2,32,256]{3,2,1,0:T(8,128)S(1)} %collective-permute-done.18.refs_1_, f32[16,2,32,256]{3,2,1,0:T(8,128)S(1)} %collective-permute-done.19.refs_2_, ...), custom_call_target="tpu_custom_call" | custom-call | flops 2097152000 | bytes 18874368 | tf_op jit(solution)/shard_map/step_last/pallas_call | solution.py:219
  354.7 1.3 copy-done.6
  356.5 1.6 broadcast_in_dim.66
  358.4 1.8 bitcast_dynamic-update-slice_fusion.4
  360.5 23.5 %collective-permute-done.15 = f32[8,8,32,256]{3,2,1,0:T(8,128)} collective-permute-done((f32[8,8,32,256]{3,2,1,0:T(8,128)}, f32[8,8,32,256]{3,2,1,0:T(8,128)}, u32[]{:S(2)}, u32[]{:S(2)}) %collective-permute-start.15) | collective-permute-done | bytes 2097184 | tf_op jit(solution)/shard_map/ppermute | solution.py:333
  384.0 1.8 bitcast_dynamic-update-slice_fusion.2
  386.2 41.8 %collective-permute-done.20 = f32[8,8,32,256]{3,2,1,0:T(8,128)} collective-permute-done((f32[8,8,32,256]{3,2,1,0:T(8,128)}, f32[8,8,32,256]{3,2,1,0:T(8,128)}, u32[]{:S(2)}, u32[]{:S(2)}) %collective-permute-start.20) | collective-permute-done | bytes 2097184 | tf_op jit(solution)/shard_map/ppermute | solution.py:333
  428.0 3.2 bitcast_dynamic-update-slice_fusion
  (131 shorter events, 12.2 us)
Async XLA Ops:
  0.0 19.0 %copy-start = (s32[8,64,256]{2,1,0:T(8,128)S(1)}, s32[8,64,256]{2,1,0:T(8,128)}, u32[]{:S(2)}) copy-start(s32[8,64,256]{2,1,0:T(8,128)} %param.15) | copy-start | bytes 1572868
  5.3 38.6 %collective-permute-start.1 = (f32[1,2,3,8,8,256]{5,4,3,2,1,0:T(8,128)}, f32[1,2,3,8,8,256]{5,4,3,2,1,0:T(8,128)}, u32[]{:S(2)}, u32[]{:S(2)}) collective-permute-start(f32[1,2,3,8,8,256]{5,4,3,2,1,0:T(8,128)} %maximum_select_fusion.1), channel_id=1, source_target_pairs={{0,1},{1,0},{2,3},{3,2},{4,5},{5,4},{6,7},{7,6},{8,9},{9,8},{10,11... | collective-permute-start | bytes 1179656 | tf_op jit(solution)/shard_map/ppermute | solution.py:296
  6.9 12.2 %copy-start.17 = (f32[8,64,256]{2,1,0:T(8,128)S(1)}, f32[8,64,256]{2,1,0:T(8,128)}, u32[]{:S(2)}) copy-start(f32[8,64,256]{2,1,0:T(8,128)} %param.12) | copy-start | bytes 1572868
  6.9 13.1 %copy-start.22 = (f32[3,8,16]{2,1,0:T(8,128)S(1)}, f32[3,8,16]{2,1,0:T(8,128)}, u32[]{:S(2)}) copy-start(f32[3,8,16]{2,1,0:T(8,128)} %param.14) | copy-start | bytes 4612
  6.9 13.1 %copy-start.23 = (f32[24,16,1]{0,1,2:T(8,128)S(1)}, f32[24,16,1]{0,1,2:T(8,128)}, u32[]{:S(2)}) copy-start(f32[24,16,1]{0,1,2:T(8,128)} %constant.130) | copy-start | bytes 4612
  16.5 237.1 %collective-permute-start.14 = (f32[8,8,32,256]{3,2,1,0:T(8,128)}, f32[8,8,32,256]{3,2,1,0:T(8,128)}, u32[]{:S(2)}, u32[]{:S(2)}) collective-permute-start(f32[8,8,32,256]{3,2,1,0:T(8,128)} %get-tuple-element.47), channel_id=1, source_target_pairs={{0,1},{1,0},{2,3},{3,2},{4,5},{5,4},{6,7},{7,6},{8,9},{9,8},{10,11... | collective-permute-start | bytes 6291464 | tf_op jit(solution)/shard_map/ppermute | solution.py:302
  17.0 181.1 %collective-permute-start.8 = (f32[8,8,32,256]{3,2,1,0:T(8,128)}, f32[8,8,32,256]{3,2,1,0:T(8,128)}, u32[]{:S(2)}, u32[]{:S(2)}) collective-permute-start(f32[8,8,32,256]{3,2,1,0:T(8,128)} %get-tuple-element.49), channel_id=1, source_target_pairs={{0,1},{1,0},{2,3},{3,2},{4,5},{5,4},{6,7},{7,6},{8,9},{9,8},{10,11... | collective-permute-start | bytes 6291464 | tf_op jit(solution)/shard_map/ppermute | solution.py:302
  18.5 135.3 %collective-permute-start = (f32[8,8,32,256]{3,2,1,0:T(8,128)}, f32[8,8,32,256]{3,2,1,0:T(8,128)}, u32[]{:S(2)}, u32[]{:S(2)}) collective-permute-start(f32[8,8,32,256]{3,2,1,0:T(8,128)} %get-tuple-element.50), channel_id=1, source_target_pairs={{0,1},{1,0},{2,3},{3,2},{4,5},{5,4},{6,7},{7,6},{8,9},{9,8},{10,11... | collective-permute-start | bytes 6291464 | tf_op jit(solution)/shard_map/ppermute | solution.py:302
  33.1 6.8 %copy-start.14 = (f32[3,8,8,1,256]{4,3,2,1,0:T(1,128)S(1)}, f32[3,8,8,1,256]{4,3,2,1,0:T(1,128)}, u32[]{:S(2)}) copy-start(f32[3,8,8,1,256]{4,3,2,1,0:T(1,128)} %get-tuple-element.54) | copy-start | bytes 589828
  37.8 2.0 copy-start.15
  37.8 2.9 copy-start.16
  40.7 0.8 copy-start.13
  41.5 9.3 %copy-start.20 = (bf16[2,96,192]{2,1,0:T(8,128)(2,1)S(1)}, bf16[2,96,192]{2,1,0:T(8,128)(2,1)}, u32[]{:S(2)}) copy-start(bf16[2,96,192]{2,1,0:T(8,128)(2,1)} %constant.97.clone) | copy-start | bytes 221188
  41.5 9.3 %copy-start.21 = (bf16[2,96,192]{2,1,0:T(8,128)(2,1)S(1)}, bf16[2,96,192]{2,1,0:T(8,128)(2,1)}, u32[]{:S(2)}) copy-start(bf16[2,96,192]{2,1,0:T(8,128)(2,1)} %constant.96.clone) | copy-start | bytes 221188
  42.7 111.0 %copy-start.3 = (f32[8,8,32,256]{3,2,1,0:T(8,128)S(1)}, f32[8,8,32,256]{3,2,1,0:T(8,128)}, u32[]{:S(2)}) copy-start(f32[8,8,32,256]{3,2,1,0:T(8,128)} %get-tuple-element.26.refs_0_) | copy-start | bytes 6291460
  45.3 5.9 %collective-permute-start.2 = (f32[1,3,16,2,256]{4,3,2,1,0:T(2,128)S(1)}, f32[1,3,16,2,256]{4,3,2,1,0:T(2,128)S(1)}, u32[]{:S(2)}, u32[]{:S(2)}) collective-permute-start(f32[1,3,16,2,256]{4,3,2,1,0:T(2,128)S(1)} %get-tuple-element.86), channel_id=1, source_target_pairs={{0,2},{2,4},{4,6},{6,8},{8,10},{10,12},{12,14},{14,16},{16,18},{18... | collective-permute-start | bytes 294920 | tf_op jit(solution)/shard_map/ppermute | solution.py:292
  47.2 5.8 %collective-permute-start.3 = (f32[1,3,16,2,256]{4,3,2,1,0:T(2,128)S(1)}, f32[1,3,16,2,256]{4,3,2,1,0:T(2,128)S(1)}, u32[]{:S(2)}, u32[]{:S(2)}) collective-permute-start(f32[1,3,16,2,256]{4,3,2,1,0:T(2,128)S(1)} %get-tuple-element.87), channel_id=1, source_target_pairs={{2,0},{4,2},{6,4},{8,6},{10,8},{12,10},{14,12},{16,14},{18,16},{20... | collective-permute-start | bytes 294920 | tf_op jit(solution)/shard_map/ppermute | solution.py:293
  155.2 5.8 %copy-start.18 = (bf16[2,64,288]{2,1,0:T(8,128)(2,1)S(1)}, bf16[2,64,288]{2,1,0:T(8,128)(2,1)}, u32[]{:S(2)}) copy-start(bf16[2,64,288]{2,1,0:T(8,128)(2,1)} %constant.99.clone) | copy-start | bytes 221188
  155.2 5.8 %copy-start.19 = (bf16[2,64,288]{2,1,0:T(8,128)(2,1)S(1)}, bf16[2,64,288]{2,1,0:T(8,128)(2,1)}, u32[]{:S(2)}) copy-start(bf16[2,64,288]{2,1,0:T(8,128)(2,1)} %constant.98.clone) | copy-start | bytes 221188
  155.3 27.4 %collective-permute-start.4 = (f32[16,2,32,256]{3,2,1,0:T(8,128)S(1)}, f32[16,2,32,256]{3,2,1,0:T(8,128)S(1)}, u32[]{:S(2)}, u32[]{:S(2)}) collective-permute-start(f32[16,2,32,256]{3,2,1,0:T(8,128)S(1)} %pad_maximum_fusion), channel_id=1, source_target_pairs={{0,2},{2,4},{4,6},{6,8},{8,10},{10,12},{12,14},{14,16},{16,18},{18... | collective-permute-start | bytes 3145736 | tf_op jit(solution)/shard_map/ppermute | solution.py:292
  157.4 25.3 %collective-permute-start.5 = (f32[16,2,32,256]{3,2,1,0:T(8,128)S(1)}, f32[16,2,32,256]{3,2,1,0:T(8,128)S(1)}, u32[]{:S(2)}, u32[]{:S(2)}) collective-permute-start(f32[16,2,32,256]{3,2,1,0:T(8,128)S(1)} %pad_maximum_fusion.1), channel_id=1, source_target_pairs={{2,0},{4,2},{6,4},{8,6},{10,8},{12,10},{14,12},{16,14},{18,16},{20... | collective-permute-start | bytes 3145736 | tf_op jit(solution)/shard_map/ppermute | solution.py:293
  182.7 15.4 %copy-start.2 = (f32[8,8,32,256]{3,2,1,0:T(8,128)S(1)}, f32[8,8,32,256]{3,2,1,0:T(8,128)}, u32[]{:S(2)}) copy-start(f32[8,8,32,256]{3,2,1,0:T(8,128)} %get-tuple-element.34.refs_0_) | copy-start | bytes 6291460
  199.7 38.6 %collective-permute-start.10 = (f32[16,2,32,256]{3,2,1,0:T(8,128)S(1)}, f32[16,2,32,256]{3,2,1,0:T(8,128)S(1)}, u32[]{:S(2)}, u32[]{:S(2)}) collective-permute-start(f32[16,2,32,256]{3,2,1,0:T(8,128)S(1)} %pad_maximum_fusion.2), channel_id=1, source_target_pairs={{0,2},{2,4},{4,6},{6,8},{8,10},{10,12},{12,14},{14,16},{16,18},{18... | collective-permute-start | bytes 3145736 | tf_op jit(solution)/shard_map/ppermute | solution.py:292
  201.7 36.6 %collective-permute-start.11 = (f32[16,2,32,256]{3,2,1,0:T(8,128)S(1)}, f32[16,2,32,256]{3,2,1,0:T(8,128)S(1)}, u32[]{:S(2)}, u32[]{:S(2)}) collective-permute-start(f32[16,2,32,256]{3,2,1,0:T(8,128)S(1)} %pad_maximum_fusion.3), channel_id=1, source_target_pairs={{2,0},{4,2},{6,4},{8,6},{10,8},{12,10},{14,12},{16,14},{18,16},{20... | collective-permute-start | bytes 3145736 | tf_op jit(solution)/shard_map/ppermute | solution.py:293
  208.1 56.6 %collective-permute-start.7 = (f32[16,2,32,256]{3,2,1,0:T(8,128)S(1)}, f32[16,2,32,256]{3,2,1,0:T(8,128)S(1)}, u32[]{:S(2)}, u32[]{:S(2)}) collective-permute-start(f32[16,2,32,256]{3,2,1,0:T(8,128)S(1)} %get-tuple-element.61), channel_id=1, source_target_pairs={{2,0},{4,2},{6,4},{8,6},{10,8},{12,10},{14,12},{16,14},{18,16},{20... | collective-permute-start | bytes 3145736 | tf_op jit(solution)/shard_map/ppermute | solution.py:293
  210.0 57.1 %collective-permute-start.6 = (f32[16,2,32,256]{3,2,1,0:T(8,128)S(1)}, f32[16,2,32,256]{3,2,1,0:T(8,128)S(1)}, u32[]{:S(2)}, u32[]{:S(2)}) collective-permute-start(f32[16,2,32,256]{3,2,1,0:T(8,128)S(1)} %get-tuple-element.62), channel_id=1, source_target_pairs={{0,2},{2,4},{4,6},{6,8},{8,10},{10,12},{12,14},{14,16},{16,18},{18... | collective-permute-start | bytes 3145736 | tf_op jit(solution)/shard_map/ppermute | solution.py:292
  255.1 38.6 %collective-permute-start.16 = (f32[16,2,32,256]{3,2,1,0:T(8,128)S(1)}, f32[16,2,32,256]{3,2,1,0:T(8,128)S(1)}, u32[]{:S(2)}, u32[]{:S(2)}) collective-permute-start(f32[16,2,32,256]{3,2,1,0:T(8,128)S(1)} %pad_maximum_fusion.4), channel_id=1, source_target_pairs={{0,2},{2,4},{4,6},{6,8},{8,10},{10,12},{12,14},{14,16},{16,18},{18... | collective-permute-start | bytes 3145736 | tf_op jit(solution)/shard_map/ppermute | solution.py:292
  257.1 37.5 %collective-permute-start.17 = (f32[16,2,32,256]{3,2,1,0:T(8,128)S(1)}, f32[16,2,32,256]{3,2,1,0:T(8,128)S(1)}, u32[]{:S(2)}, u32[]{:S(2)}) collective-permute-start(f32[16,2,32,256]{3,2,1,0:T(8,128)S(1)} %pad_maximum_fusion.5), channel_id=1, source_target_pairs={{2,0},{4,2},{6,4},{8,6},{10,8},{12,10},{14,12},{16,14},{18,16},{20... | collective-permute-start | bytes 3145736 | tf_op jit(solution)/shard_map/ppermute | solution.py:293
  262.8 55.7 %collective-permute-start.13 = (f32[16,2,32,256]{3,2,1,0:T(8,128)S(1)}, f32[16,2,32,256]{3,2,1,0:T(8,128)}, u32[]{:S(2)}, u32[]{:S(2)}) collective-permute-start(f32[16,2,32,256]{3,2,1,0:T(8,128)S(1)} %get-tuple-element.59), channel_id=1, source_target_pairs={{2,0},{4,2},{6,4},{8,6},{10,8},{12,10},{14,12},{16,14},{18,16},{20... | collective-permute-start | bytes 3145736 | tf_op jit(solution)/shard_map/ppermute | solution.py:293
  264.7 53.8 %collective-permute-start.12 = (f32[16,2,32,256]{3,2,1,0:T(8,128)S(1)}, f32[16,2,32,256]{3,2,1,0:T(8,128)}, u32[]{:S(2)}, u32[]{:S(2)}) collective-permute-start(f32[16,2,32,256]{3,2,1,0:T(8,128)S(1)} %get-tuple-element.60), channel_id=1, source_target_pairs={{0,2},{2,4},{4,6},{6,8},{8,10},{10,12},{12,14},{14,16},{16,18},{18... | collective-permute-start | bytes 3145736 | tf_op jit(solution)/shard_map/ppermute | solution.py:292
  282.7 1.4 copy-start.4
  284.1 74.3 %collective-permute-start.9 = (f32[8,8,32,256]{3,2,1,0:T(8,128)}, f32[8,8,32,256]{3,2,1,0:T(8,128)}, u32[]{:S(2)}, u32[]{:S(2)}) collective-permute-start(f32[8,8,32,256]{3,2,1,0:T(8,128)} %get-tuple-element.33), channel_id=1, source_target_pairs={{0,1},{1,0},{2,3},{3,2},{4,5},{5,4},{6,7},{7,6},{8,9},{9,8},{10,11... | collective-permute-start | bytes 6291464 | tf_op jit(solution)/shard_map/ppermute | solution.py:333
  293.7 1.0 copy-start.8
  294.6 1.0 copy-start.10
  295.6 1.2 copy-start.9
  296.8 1.2 copy-start.11
  313.6 25.5 %collective-permute-start.19 = (f32[16,2,32,256]{3,2,1,0:T(8,128)S(1)}, f32[16,2,32,256]{3,2,1,0:T(8,128)S(1)}, u32[]{:S(2)}, u32[]{:S(2)}) collective-permute-start(f32[16,2,32,256]{3,2,1,0:T(8,128)S(1)} %get-tuple-element.57), channel_id=1, source_target_pairs={{2,0},{4,2},{6,4},{8,6},{10,8},{12,10},{14,12},{16,14},{18,16},{20... | collective-permute-start | bytes 3145736 | tf_op jit(solution)/shard_map/ppermute | solution.py:293
  315.5 23.5 %collective-permute-start.18 = (f32[16,2,32,256]{3,2,1,0:T(8,128)S(1)}, f32[16,2,32,256]{3,2,1,0:T(8,128)S(1)}, u32[]{:S(2)}, u32[]{:S(2)}) collective-permute-start(f32[16,2,32,256]{3,2,1,0:T(8,128)S(1)} %get-tuple-element.58), channel_id=1, source_target_pairs={{0,2},{2,4},{4,6},{6,8},{8,10},{10,12},{12,14},{14,16},{16,18},{18... | collective-permute-start | bytes 3145736 | tf_op jit(solution)/shard_map/ppermute | solution.py:292
  335.1 48.9 %collective-permute-start.15 = (f32[8,8,32,256]{3,2,1,0:T(8,128)}, f32[8,8,32,256]{3,2,1,0:T(8,128)}, u32[]{:S(2)}, u32[]{:S(2)}) collective-permute-start(f32[8,8,32,256]{3,2,1,0:T(8,128)} %get-tuple-element.40), channel_id=1, source_target_pairs={{0,1},{1,0},{2,3},{3,2},{4,5},{5,4},{6,7},{7,6},{8,9},{9,8},{10,11... | collective-permute-start | bytes 6291464 | tf_op jit(solution)/shard_map/ppermute | solution.py:333
  354.7 1.3 copy-start.6
  356.0 72.0 %collective-permute-start.20 = (f32[8,8,32,256]{3,2,1,0:T(8,128)}, f32[8,8,32,256]{3,2,1,0:T(8,128)}, u32[]{:S(2)}, u32[]{:S(2)}) collective-permute-start(f32[8,8,32,256]{3,2,1,0:T(8,128)} %get-tuple-element.46), channel_id=1, source_target_pairs={{0,1},{1,0},{2,3},{3,2},{4,5},{5,4},{6,7},{7,6},{8,9},{9,8},{10,11... | collective-permute-start | bytes 6291464 | tf_op jit(solution)/shard_map/ppermute | solution.py:333
  356.5 1.6 copy-start.5
  360.5 25.4 %copy-start.7 = (f32[8,8,32,256]{3,2,1,0:T(8,128)S(1)}, f32[8,8,32,256]{3,2,1,0:T(8,128)}, u32[]{:S(2)}) copy-start(f32[8,8,32,256]{3,2,1,0:T(8,128)} %copy-done.6) | copy-start | bytes 6291460
  385.9 45.3 %copy-start.1 = (s32[8,64,256]{2,1,0:T(8,128)S(1)}, s32[8,64,256]{2,1,0:T(8,128)}, u32[]{:S(2)}) copy-start(s32[8,64,256]{2,1,0:T(8,128)} %param.15) | copy-start | bytes 1572868
  386.2 41.9 %copy-start.12 = (f32[3,8,8,64,256]{4,3,2,1,0:T(8,128)}, f32[3,8,8,64,256]{4,3,2,1,0:T(8,128)S(1)}, u32[]{:S(2)}) copy-start(f32[3,8,8,64,256]{4,3,2,1,0:T(8,128)S(1)} %bitcast_dynamic-update-slice_fusion.1) | copy-start | bytes 37748740
